TPU v7x, 512 devices: a whole 4x8x8 slice. The times are simulated.
512 devices in a mesh: gx: 32 (over x_hi, y, core), gy: 16 (over z, x_lo).
Axes of the slice: x: 4 (x_hi: 2, x_lo: 2; x = x_hi * 2 + x_lo), y: 8, z: 8, core: 2. Of those that a mesh axis runs over, the one named last changes fastest.
Arguments:
- node_features: bfloat16 [64, 32, 64, 512], P('gx', 'gy'), may hold values from -6 to 6
- edge_features: bfloat16 [3, 64, 32, 64, 512], P(None, 'gx', 'gy'), may hold values from -6 to 6
- open_faces: int32 [3, 64, 32, 64], P(None, 'gx', 'gy'), may hold values 0 or 1
- edge_weight: bfloat16 [1536, 512], replicated, may hold values from -0.15625 to 0.15625
- node_weight: bfloat16 [512, 512], replicated, may hold values from -0.25 to 0.25
- cotangent: bfloat16 [64, 32, 64, 512], P('gx', 'gy'), may hold values from -6 to 6
Outputs:
- new_nodes: bfloat16 [64, 32, 64, 512], P('gx', 'gy')
- node_grad: bfloat16 [64, 32, 64, 512], P('gx', 'gy')
- edge_weight_grad: float32 [786432], P(('gx', 'gy'))
- node_weight_grad: float32 [262144], P(('gx', 'gy'))
All inputs are finite; a program needn't handle non-finite values. No bound on the sum of `open_faces` on one device may be relied on, other than what follows from the above.
Results may differ from a plain program's by a relative error of at most 0.013.
Values may be sent and summed in bfloat16 or wider, within the bound.
A program may use at most 64 MiB of HBM per device.

v0:
```python
import jax
import jax.numpy as jnp
from jax import lax
from jax.sharding import PartitionSpec as P


def passed_along(value, axis, steps):
    count = lax.axis_size(axis)
    first, last = (max(0, -steps), min(count, count - steps))
    return lax.ppermute(value, axis, [(source, source + steps) for source in range(first, last)])


def silu_slope(values):
    sigmoid = jax.nn.sigmoid(values)
    return sigmoid * (1.0 + values * (1.0 - sigmoid))


def local(node_features, edge_features, open_faces, edge_weight, node_weight, cotangent):
    extent_first, extent_second, depth, features = node_features.shape
    total_first = extent_first * lax.axis_size("gx")
    total_second = extent_second * lax.axis_size("gy")
    place_first = lax.axis_index("gx") * extent_first + jnp.arange(extent_first)
    place_second = lax.axis_index("gy") * extent_second + jnp.arange(extent_second)
    inside_first = (place_first < total_first - 1).astype(jnp.float32)
    inside_second = (place_second < total_second - 1).astype(jnp.float32)
    inside_third = (jnp.arange(depth) < depth - 1).astype(jnp.float32)
    masks = open_faces.astype(jnp.float32)
    open_first = masks[0] * inside_first[:, None, None]
    open_second = masks[1] * inside_second[None, :, None]
    open_third = masks[2] * inside_third[None, None, :]
    open_all = jnp.stack([open_first, open_second, open_third])
    upper_first = passed_along(node_features[0:1], "gx", -1)
    upper_second = passed_along(node_features[:, 0:1], "gy", -1)
    zero_plane = jnp.zeros((extent_first, extent_second, 1, features), jnp.bfloat16)
    beside = [
        jnp.concatenate([node_features[1:], upper_first], axis=0),
        jnp.concatenate([node_features[:, 1:], upper_second], axis=1),
        jnp.concatenate([node_features[:, :, 1:], zero_plane], axis=2),
    ]
    inputs_all = jnp.concatenate(
        [
            jnp.concatenate([node_features, beside[direction], edge_features[direction]], axis=-1)
            for direction in range(3)
        ],
        axis=0,
    )
    flat_inputs = inputs_all.reshape(-1, 3 * features)
    preact = jnp.dot(flat_inputs, edge_weight, preferred_element_type=jnp.float32)
    preact = preact.reshape(3, extent_first, extent_second, depth, features)
    message = (jax.nn.silu(preact) * open_all[..., None]).astype(jnp.bfloat16)
    widened = message.astype(jnp.float32)
    zero_wide = jnp.zeros((extent_first, extent_second, 1, features), jnp.float32)
    summed = widened[0] + widened[1] + widened[2]
    summed = summed - jnp.concatenate([zero_wide, widened[2, :, :, :-1]], axis=2)
    from_first = passed_along(message[0, -1:], "gx", 1)
    from_second = passed_along(message[1, :, -1:], "gy", 1)
    entering_first = from_first.astype(jnp.float32)
    entering_second = from_second.astype(jnp.float32)
    summed = summed - jnp.concatenate([entering_first, widened[0, :-1]], axis=0)
    summed = summed - jnp.concatenate([entering_second, widened[1, :, :-1]], axis=1)
    summed_half = summed.astype(jnp.bfloat16)
    flat_summed = summed_half.reshape(-1, features)
    update = jnp.dot(flat_summed, node_weight, preferred_element_type=jnp.float32).reshape(
        node_features.shape
    )
    new_nodes = (node_features.astype(jnp.float32) + jax.nn.silu(update)).astype(jnp.bfloat16)
    grad_update = (cotangent.astype(jnp.float32) * silu_slope(update)).astype(jnp.bfloat16)
    flat_update = grad_update.reshape(-1, features)
    node_weight_grad = lax.dot_general(
        flat_summed, flat_update, (((0,), (0,)), ((), ())), preferred_element_type=jnp.float32
    )
    node_flat = node_weight_grad.reshape(-1)
    grad_summed = lax.dot_general(
        flat_update, node_weight, (((1,), (1,)), ((), ())), preferred_element_type=jnp.float32
    )
    grad_summed = grad_summed.reshape(node_features.shape).astype(jnp.bfloat16)
    grad_upper_first = passed_along(grad_summed[0:1], "gx", -1)
    grad_upper_second = passed_along(grad_summed[:, 0:1], "gy", -1)
    beside_grad = jnp.stack(
        [
            jnp.concatenate([grad_summed[1:], grad_upper_first], axis=0),
            jnp.concatenate([grad_summed[:, 1:], grad_upper_second], axis=1),
            jnp.concatenate([grad_summed[:, :, 1:], zero_plane], axis=2),
        ]
    )
    grad_message = grad_summed.astype(jnp.float32)[None] - beside_grad.astype(jnp.float32)
    grad_preact = (grad_message * open_all[..., None] * silu_slope(preact)).astype(jnp.bfloat16)
    flat_grad = grad_preact.reshape(-1, features)
    edge_weight_grad = lax.dot_general(
        flat_inputs, flat_grad, (((0,), (0,)), ((), ())), preferred_element_type=jnp.float32
    )
    backward = lax.dot_general(
        flat_grad,
        edge_weight[: 2 * features],
        (((1,), (1,)), ((), ())),
        preferred_element_type=jnp.float32,
    )
    backward = backward.reshape(3, extent_first, extent_second, depth, 2 * features)
    own_terms = backward[..., :features]
    toward = backward[..., features:]
    node_grad = cotangent.astype(jnp.float32) + own_terms[0] + own_terms[1] + own_terms[2]
    node_grad = node_grad + jnp.concatenate([zero_wide, toward[2, :, :, :-1]], axis=2)
    lower_first = passed_along(toward[0, -1:].astype(jnp.bfloat16), "gx", 1).astype(jnp.float32)
    lower_second = passed_along(toward[1, :, -1:].astype(jnp.bfloat16), "gy", 1).astype(jnp.float32)
    node_grad = node_grad + jnp.concatenate([lower_first, toward[0, :-1]], axis=0)
    node_grad = node_grad + jnp.concatenate([lower_second, toward[1, :, :-1]], axis=1)
    edge_flat = edge_weight_grad.reshape(-1)
    edge_part, node_part = (
        lax.psum_scatter(edge_flat, ("gx", "gy"), scatter_dimension=0, tiled=True),
        lax.psum_scatter(node_flat, ("gx", "gy"), scatter_dimension=0, tiled=True),
    )
    return (new_nodes, node_grad.astype(jnp.bfloat16), edge_part, node_part)


def solution(mesh):
    placed = (
        P("gx", "gy", None, None),
        P(None, "gx", "gy", None, None),
        P(None, "gx", "gy", None),
        P(),
        P(),
        P("gx", "gy", None, None),
    )
    return jax.shard_map(
        local,
        mesh=mesh,
        in_specs=placed,
        out_specs=(
            P("gx", "gy", None, None),
            P("gx", "gy", None, None),
            P(("gx", "gy")),
            P(("gx", "gy")),
        ),
        check_vma=False,
    )
```

profile of v0, /device:TPU:1, one launch (start us, length us, event | category | flops | bytes accessed | tf_op | source)
XLA Modules:
  0.0 351.7 jit_solution(18204567073697057760)
XLA Ops:
  7.2 0.0 copy-start
  7.2 0.0 copy-start.1
  7.2 0.0 all-reduce.9.cloned.1.call-start
  7.2 1.1 fusion.34
  8.3 1.3 collective-permute-start.1
  9.6 1.0 fusion.33
  10.6 8.7 %collective-permute-start = (bf16[1,2,64,512]{3,2,1,0:T(8,128)(2,1)S(1)}, bf16[1,2,64,512]{3,2,1,0:T(8,128)(2,1)S(1)}, u32[]{:S(2)}, u32[]{:S(2)}) collective-permute-start(bf16[1,2,64,512]{3,2,1,0:T(8,128)(2,1)S(1)} %get-tuple-element.16), channel_id=1, source_target_pairs={{16,0},{32,16},{48,32},{64,48},{80,64},{96,80},{112,96},{128,112},... | collective-permute-start | bytes 393224 | tf_op jit(solution)/shard_map/ppermute | solution.py:10
  19.4 0.7 convert_element_type.98
  20.1 1.2 slice_bitcast_fusion.11
  21.2 0.1 slice_multiply_fusion.2
  21.3 0.0 copy-done.1
  21.3 0.0 copy-start.2
  21.3 0.1 slice.117
  21.4 0.0 collective-permute-done.1
  21.4 0.0 collective-permute-done
  21.4 0.3 fusion.6
  21.7 1.0 copy-done.2
  22.7 1.6 fusion.30
  24.4 1.9 collective-permute-start.2
  26.4 4.3 %collective-permute-start.3 = (bf16[2,1,64,512]{3,2,0,1:T(8,128)(2,1)S(1)}, bf16[2,1,64,512]{3,2,0,1:T(8,128)(2,1)S(1)}, u32[]{:S(2)}, u32[]{:S(2)}) collective-permute-start(bf16[2,1,64,512]{3,2,0,1:T(8,128)(2,1)S(1)} %slice_bitcast_fusion.14), channel_id=1, source_target_pairs={{0,1},{1,2},{2,3},{3,4},{4,5},{5,6},{6,7},{7,8},{8,9},{9,10},{10,1... | collective-permute-start | bytes 393224 | tf_op jit(solution)/shard_map/ppermute | solution.py:10
  30.7 0.0 collective-permute-done.2
  30.7 2.3 collective-permute-done.3
  33.0 0.4 fusion.22
  33.4 0.0 copy-done
  33.4 0.0 copy-start.3
  33.4 1.1 add_convert_fusion
  34.5 0.0 copy-done.3
  34.5 0.4 fusion.35
  34.9 0.5 convolution_bitcast_fusion.1
  35.4 1.3 collective-permute-start.5
  36.7 0.1 slice.159
  36.8 3.3 collective-permute-start.4
  40.1 1.3 copy.25
  41.4 0.4 collective-permute-done.5
  41.9 1.5 collective-permute-done.4
  43.4 0.7 multiply_convert_fusion
  44.1 1.4 convolution_bitcast_fusion
  45.6 2.5 copy.24
  48.1 0.0 all-reduce.9.cloned.1.call-update
  48.1 1.0 fusion.9
  49.1 1.9 collective-permute-start.6
  51.1 4.7 %collective-permute-start.7 = (bf16[2,1,64,512]{3,2,1,0:T(8,128)(2,1)S(1)}, bf16[2,1,64,512]{3,2,1,0:T(8,128)(2,1)S(1)}, u32[]{:S(2)}, u32[]{:S(2)}) collective-permute-start(bf16[2,1,64,512]{3,2,1,0:T(8,128)(2,1)S(1)} %slice_bitcast_fusion.12), channel_id=1, source_target_pairs={{0,1},{1,2},{2,3},{3,4},{4,5},{5,6},{6,7},{7,8},{8,9},{9,10},{10,1... | collective-permute-start | bytes 393224 | tf_op jit(solution)/shard_map/ppermute | solution.py:10
  55.9 0.0 collective-permute-done.6
  56.0 3.6 %collective-permute-done.7 = bf16[2,1,64,512]{3,2,1,0:T(8,128)(2,1)S(1)} collective-permute-done((bf16[2,1,64,512]{3,2,1,0:T(8,128)(2,1)S(1)}, bf16[2,1,64,512]{3,2,1,0:T(8,128)(2,1)S(1)}, u32[]{:S(2)}, u32[]{:S(2)}) %collective-permute-start.7) | collective-permute-done | bytes 131104 | tf_op jit(solution)/shard_map/ppermute | solution.py:10
  59.6 1.1 fusion.18
  60.7 281.4 %all-reduce.9.cloned.1.call-done = (f32[786432]{0:T(1024)}, f32[262144]{0:T(1024)}) async-done(((f32[786432]{0:T(1024)}, f32[262144]{0:T(1024)}), (f32[786432]{0:T(1024)}, f32[262144]{0:T(1024)})) %all-reduce.9.cloned.1.call-update) | async-done | bytes 4194320
  342.1 1.4 dynamic-slice
  343.5 1.3 dynamic-slice.1
  (22 shorter events, 0.4 us)
Async XLA Ops:
  7.2 26.2 %copy-start = (bf16[512,512]{1,0:T(8,128)(2,1)S(1)}, bf16[512,512]{1,0:T(8,128)(2,1)}, u32[]{:S(2)}) copy-start(bf16[512,512]{1,0:T(8,128)(2,1)} %param.10) | copy-start | bytes 1572868
  7.2 14.1 %copy-start.1 = (bf16[2,2,64,512]{3,2,1,0:T(8,128)(2,1)S(1)}, bf16[2,2,64,512]{3,2,1,0:T(8,128)(2,1)}, u32[]{:S(2)}) copy-start(bf16[2,2,64,512]{3,2,1,0:T(8,128)(2,1)} %param.6) | copy-start | bytes 786436
  7.2 334.9 %all-reduce.9.cloned.1.call-start = ((), (), s32[]{:S(2)}) async-start(), calls=%async_computation | async-start | bytes 8388608
  8.3 13.1 %collective-permute-start.1 = (bf16[2,1,64,512]{3,2,1,0:T(8,128)(2,1)S(1)}, bf16[2,1,64,512]{3,2,1,0:T(8,128)(2,1)S(1)}, u32[]{:S(2)}, u32[]{:S(2)}) collective-permute-start(bf16[2,1,64,512]{3,2,1,0:T(8,128)(2,1)S(1)} %get-tuple-element.18), channel_id=1, source_target_pairs={{1,0},{2,1},{3,2},{4,3},{5,4},{6,5},{7,6},{8,7},{9,8},{10,9},{11,1... | collective-permute-start | bytes 393224 | tf_op jit(solution)/shard_map/ppermute | solution.py:10
  10.6 10.8 %collective-permute-start = (bf16[1,2,64,512]{3,2,1,0:T(8,128)(2,1)S(1)}, bf16[1,2,64,512]{3,2,1,0:T(8,128)(2,1)S(1)}, u32[]{:S(2)}, u32[]{:S(2)}) collective-permute-start(bf16[1,2,64,512]{3,2,1,0:T(8,128)(2,1)S(1)} %get-tuple-element.16), channel_id=1, source_target_pairs={{16,0},{32,16},{48,32},{64,48},{80,64},{96,80},{112,96},{128,112},... | collective-permute-start | bytes 393224 | tf_op jit(solution)/shard_map/ppermute | solution.py:10
  21.3 1.4 copy-start.2
  24.4 6.2 %collective-permute-start.2 = (bf16[1,2,64,512]{3,2,0,1:T(8,128)(2,1)S(1)}, bf16[1,2,64,512]{3,2,0,1:T(8,128)(2,1)S(1)}, u32[]{:S(2)}, u32[]{:S(2)}) collective-permute-start(bf16[1,2,64,512]{3,2,0,1:T(8,128)(2,1)S(1)} %slice_bitcast_fusion.15), channel_id=1, source_target_pairs={{0,16},{16,32},{32,48},{48,64},{64,80},{80,96},{96,112},{112,128},... | collective-permute-start | bytes 393224 | tf_op jit(solution)/shard_map/ppermute | solution.py:10
  26.4 6.6 %collective-permute-start.3 = (bf16[2,1,64,512]{3,2,0,1:T(8,128)(2,1)S(1)}, bf16[2,1,64,512]{3,2,0,1:T(8,128)(2,1)S(1)}, u32[]{:S(2)}, u32[]{:S(2)}) collective-permute-start(bf16[2,1,64,512]{3,2,0,1:T(8,128)(2,1)S(1)} %slice_bitcast_fusion.14), channel_id=1, source_target_pairs={{0,1},{1,2},{2,3},{3,4},{4,5},{5,6},{6,7},{7,8},{8,9},{9,10},{10,1... | collective-permute-start | bytes 393224 | tf_op jit(solution)/shard_map/ppermute | solution.py:10
  33.4 1.1 copy-start.3
  35.4 6.5 %collective-permute-start.5 = (bf16[2,1,64,512]{3,2,1,0:T(8,128)(2,1)S(1)}, bf16[2,1,64,512]{3,2,1,0:T(8,128)(2,1)S(1)}, u32[]{:S(2)}, u32[]{:S(2)}) collective-permute-start(bf16[2,1,64,512]{3,2,1,0:T(8,128)(2,1)S(1)} %get-tuple-element.14), channel_id=1, source_target_pairs={{1,0},{2,1},{3,2},{4,3},{5,4},{6,5},{7,6},{8,7},{9,8},{10,9},{11,1... | collective-permute-start | bytes 393224 | tf_op jit(solution)/shard_map/ppermute | solution.py:10
  36.8 6.6 %collective-permute-start.4 = (bf16[1,2,64,512]{3,2,1,0:T(8,128)(2,1)S(1)}, bf16[1,2,64,512]{3,2,1,0:T(8,128)(2,1)S(1)}, u32[]{:S(2)}, u32[]{:S(2)}) collective-permute-start(bf16[1,2,64,512]{3,2,1,0:T(8,128)(2,1)S(1)} %get-tuple-element.12), channel_id=1, source_target_pairs={{16,0},{32,16},{48,32},{64,48},{80,64},{96,80},{112,96},{128,112},... | collective-permute-start | bytes 393224 | tf_op jit(solution)/shard_map/ppermute | solution.py:10
  49.1 6.8 %collective-permute-start.6 = (bf16[1,2,64,512]{3,2,1,0:T(8,128)(2,1)S(1)}, bf16[1,2,64,512]{3,2,1,0:T(8,128)(2,1)S(1)}, u32[]{:S(2)}, u32[]{:S(2)}) collective-permute-start(bf16[1,2,64,512]{3,2,1,0:T(8,128)(2,1)S(1)} %slice_bitcast_fusion.13), channel_id=1, source_target_pairs={{0,16},{16,32},{32,48},{48,64},{64,80},{80,96},{96,112},{112,128},... | collective-permute-start | bytes 393224 | tf_op jit(solution)/shard_map/ppermute | solution.py:10
  51.1 8.5 %collective-permute-start.7 = (bf16[2,1,64,512]{3,2,1,0:T(8,128)(2,1)S(1)}, bf16[2,1,64,512]{3,2,1,0:T(8,128)(2,1)S(1)}, u32[]{:S(2)}, u32[]{:S(2)}) collective-permute-start(bf16[2,1,64,512]{3,2,1,0:T(8,128)(2,1)S(1)} %slice_bitcast_fusion.12), channel_id=1, source_target_pairs={{0,1},{1,2},{2,3},{3,4},{4,5},{5,6},{6,7},{7,8},{8,9},{9,10},{10,1... | collective-permute-start | bytes 393224 | tf_op jit(solution)/shard_map/ppermute | solution.py:10
Sparse Core Ops, SparseCore 0:
  48.2 293.8 all-reduce.8
where the time goes:
time: 353 us; the launch traced here: 352 us
  waiting for transfers between devices  289 us (82%)
  starting transfers between devices  27.5 us (8%)
  between operations  14.4 us (4%)
  local copies, waits for them, and re-layouts  11.2 us (3%)
  matrix products  6.01 us (2%)
    unnamed x2, waiting for transfers between devices  281 us
    ppermute x8, starting transfers between devices, passed_along(): lax.ppermute(value, axis, [(source, source + steps) for source in range(f...  27.4 us
    ppermute x8, waiting for transfers between devices, passed_along(): lax.ppermute(value, axis, [(source, source + steps) for source in range(f...  7.8 us
    unnamed x12, local copies, waits for them, and re-layouts  7.55 us
  transfers between devices with their start and end apart: 9, of which 5 were waited for; matrix products, arithmetic and copies ran while one was open for 2% of the time, Pallas kernels for 0%

commit v1 on v0

--- a/solution.py
+++ b/solution.py
@@ -1,6 +1,8 @@
 import jax
 import jax.numpy as jnp
 from jax import lax
+from jax.experimental import pallas as pl
+from jax.experimental.pallas import tpu as pltpu
 from jax.sharding import PartitionSpec as P
 
 
@@ -13,6 +15,226 @@
 def silu_slope(values):
     sigmoid = jax.nn.sigmoid(values)
     return sigmoid * (1.0 + values * (1.0 - sigmoid))
+
+
+MESH = pl.DeviceIdType.MESH
+BF = jnp.bfloat16
+F32 = jnp.float32
+
+
+class Place:
+    def __init__(self):
+        gx, gy = lax.axis_index("gx"), lax.axis_index("gy")
+        self.gx, self.gy = gx, gy
+        self.x_hi, self.y, self.core = gx // 16, (gx // 2) % 8, gx % 2
+        self.z, self.x_lo = gy // 2, gy % 2
+        self.x = self.x_hi * 2 + self.x_lo
+        self.sibling = (gx + 1 - 2 * self.core, gy)
+
+    def along(self, axis, step):
+        if axis == "x":
+            other = (self.x + step) % 4
+            return other, ((other // 2) * 16 + self.y * 2 + self.core, self.z * 2 + other % 2)
+        if axis == "y":
+            other = (self.y + step) % 8
+            return other, (self.x_hi * 16 + other * 2 + self.core, self.gy)
+        other = (self.z + step) % 8
+        return other, (self.gx, other * 2 + self.x_lo)
+
+    def partners(self):
+        found = [self.sibling]
+        for axis, count in (("x", 4), ("y", 8), ("z", 8)):
+            found += [self.along(axis, step)[1] for step in range(1, count)]
+        return found
+
+
+def greet(devices):
+    barrier = pltpu.get_barrier_semaphore()
+    for device in devices:
+        pl.semaphore_signal(barrier, inc=1, device_id=device, device_id_type=MESH)
+    pl.semaphore_wait(barrier, len(devices))
+
+
+def push(source, target, send_sem, recv_sem, device):
+    copy = pltpu.make_async_remote_copy(
+        src_ref=source, dst_ref=target, send_sem=send_sem, recv_sem=recv_sem, device_id=device, device_id_type=MESH
+    )
+    copy.start()
+    return copy
+
+
+SIZES = {"x": 4, "y": 8, "z": 8}
+FAR = {4: (2, 1, 3), 8: (4, 3, 5, 2, 6, 1, 7)}
+ORDERS = (("x", "y", "z"), ("y", "x", "z"), ("z", "x", "y"), ("x", "z", "y"))
+TYPES = {0: (0, 0), 1: (0, 1), 3: (1, 0), 2: (1, 1)}
+
+
+def scatter_scratch():
+    shapes = []
+    for first, second, _ in ORDERS:
+        one, two = SIZES[first], SIZES[second]
+        shapes += [pltpu.VMEM((one, 2, two, 16, 128), BF)] * 2
+        shapes += [pltpu.VMEM((two, 2, 16, 128), BF)] * 2
+    shapes += [pltpu.VMEM((2, 64, 128), F32)]
+    shapes += [pltpu.VMEM((2, 8, 8, 128), F32)] * 2
+    shapes += [pltpu.VMEM((2, 8, 128), F32)] * 2
+    shapes += [pltpu.SemaphoreType.DMA((4, 8))] * 4 + [pltpu.SemaphoreType.DMA((2, 8))] * 2
+    shapes += [pltpu.SemaphoreType.DMA] * 2
+    return shapes
+
+
+def fill_first(place, plane, step, edge, node, out):
+    first, second, _ = ORDERS[plane]
+    dest, device = place.along(first, step)
+    for c in range(2):
+        if plane == 0:
+            start = 768 * (dest // 2) + 3 * (dest % 2)
+            rows = edge[c, pl.ds(start, 128, stride=6), :]
+            out[step, c] = rows.astype(BF).reshape(8, 16, 128)
+        elif plane == 1:
+            for hi in range(2):
+                for lo in range(2):
+                    start = 768 * hi + 3 * lo + 1 + 96 * dest
+                    out[step, c, 2 * hi + lo] = edge[c, pl.ds(start, 16, stride=6), :].astype(BF)
+        elif plane == 2:
+            for hi in range(2):
+                for lo in range(2):
+                    start = 768 * hi + 3 * lo + 2 + 6 * dest
+                    rows = [edge[c, pl.ds(start + 48 * core, 8, stride=96), :] for core in range(2)]
+                    out[step, c, 2 * hi + lo] = jnp.concatenate(rows, axis=0).astype(BF)
+        else:
+            for high in range(8):
+                start = 256 * (dest // 2) + dest % 2 + 2 * high
+                rows = [node[c, pl.ds(start + 16 * core, 8, stride=32), :] for core in range(2)]
+                out[step, c, high] = jnp.concatenate(rows, axis=0).astype(BF)
+    return device
+
+
+def scatter(place, edge, node, scratch, planes_first=(1, 2, 0, 3)):
+    bufs = [scratch[4 * plane: 4 * plane + 4] for plane in range(4)]
+    wide, send_three, recv_three, last, last_in = scratch[16:21]
+    send_1, recv_1, send_2, recv_2, send_3, recv_3, send_4, recv_4 = scratch[21:29]
+    stage_1 = {plane: {} for plane in range(4)}
+    stage_2 = {plane: {} for plane in range(4)}
+    for plane in planes_first:
+        first = ORDERS[plane][0]
+        out, landing = bufs[plane][:2]
+        for step in FAR[SIZES[first]]:
+            device = fill_first(place, plane, step, edge, node, out)
+            stage_1[plane][step] = push(out.at[step], landing.at[step], send_1.at[plane, step], recv_1.at[plane, step], device)
+        fill_first(place, plane, 0, edge, node, out)
+    for plane in planes_first:
+        first, second, _ = ORDERS[plane]
+        out, landing, out_2, landing_2 = bufs[plane]
+        for step in (1, 7, 2, 6, 3, 5, 4) if SIZES[first] == 8 else (1, 3, 2):
+            stage_1[plane][step].wait_recv()
+        for step in FAR[SIZES[second]] + (0,):
+            dest, device = place.along(second, step)
+            total = out[0, :, dest].astype(F32)
+            for source in range(1, SIZES[first]):
+                total = total + landing[source, :, dest].astype(F32)
+            out_2[step] = total.astype(BF)
+            if step:
+                stage_2[plane][step] = push(out_2.at[step], landing_2.at[step], send_2.at[plane, step], recv_2.at[plane, step], device)
+    stage_3 = []
+    for kind, axis in ((0, "z"), (1, "y")):
+        for plane in range(4):
+            if TYPES[plane][0] != kind:
+                continue
+            out_2, landing_2 = bufs[plane][2:]
+            count = SIZES[ORDERS[plane][1]]
+            for step in range(1, count):
+                stage_2[plane][step].wait_recv()
+            total = out_2[0].astype(F32)
+            for source in range(1, count):
+                total = total + landing_2[source].astype(F32)
+            slot = TYPES[plane][1]
+            for c in range(2):
+                for core in range(2):
+                    row = (core * 4 + slot * 2 + c) * 8
+                    wide[kind, pl.ds(row, 8), :] = total[c, core * 8: core * 8 + 8]
+        for step in FAR[8] + (0,):
+            dest, device = place.along(axis, step)
+            send_three[kind, step] = wide[kind, pl.ds(dest, 8, stride=8), :]
+            if step:
+                stage_3.append(push(send_three.at[kind, step], recv_three.at[kind, step], send_3.at[kind, step], recv_3.at[kind, step], device))
+    for copy in stage_3:
+        copy.wait_recv()
+    for kind in range(2):
+        total = send_three[kind, 0]
+        for step in range(1, 8):
+            total = total + recv_three[kind, step]
+        last[kind] = total
+    swap = push(last, last_in, send_4, recv_4, place.sibling)
+    swap.wait_recv()
+    pending = stage_3 + [swap]
+    for plane in range(4):
+        pending += list(stage_1[plane].values()) + list(stage_2[plane].values())
+
+    def finish(edge_out, node_out):
+        for plane in range(4):
+            kind, slot = TYPES[plane]
+            rows = pl.ds(place.core * 4 + slot * 2, 2)
+            mine, theirs = last[kind, rows, :], last_in[kind, rows, :]
+            low = jnp.where(place.core == 0, mine, theirs)
+            high = jnp.where(place.core == 0, theirs, mine)
+            if plane < 3:
+                edge_out[pl.ds(4 * plane, 2), :] = low
+                edge_out[pl.ds(4 * plane + 2, 2), :] = high
+            else:
+                node_out[pl.ds(0, 2), :] = low
+                node_out[pl.ds(2, 2), :] = high
+        for copy in pending:
+            copy.wait_send()
+
+    return finish
+
+
+def reduce_kernel(edge_in, node_in, edge_out, node_out, edge, node, edge_to, edge_from, node_to, node_from, swap_send, swap_recv, *scratch):
+    place = Place()
+    mine = pl.multiple_of(place.core * 256, 256)
+    other = pl.multiple_of(256 - place.core * 256, 256)
+    greet(place.partners())
+    node_to[...] = node_in[:, pl.ds(other, 256)].astype(BF)
+    swaps = [push(node_to, node_from, swap_send.at[3], swap_recv.at[3], place.sibling)]
+    for part in range(3):
+        rows = pl.ds(512 * part, 512)
+        edge_to[part] = edge_in[rows, pl.ds(other, 256)].astype(BF)
+        swaps.append(push(edge_to.at[part], edge_from.at[part], swap_send.at[part], swap_recv.at[part], place.sibling))
+    swaps[0].wait_recv()
+    for c in range(2):
+        node[c] = node_in[:, pl.ds(pl.multiple_of(mine + 128 * c, 128), 128)] + node_from[:, 128 * c: 128 * c + 128].astype(F32)
+    for part in range(3):
+        swaps[part + 1].wait_recv()
+        for c in range(2):
+            edge[c, pl.ds(512 * part, 512), :] = edge_in[pl.ds(512 * part, 512), pl.ds(pl.multiple_of(mine + 128 * c, 128), 128)] + edge_from[part, :, 128 * c: 128 * c + 128].astype(F32)
+    finish = scatter(place, edge, node, scratch)
+    finish(edge_out, node_out)
+    for copy in swaps:
+        copy.wait_send()
+
+
+def reduce_scatter(edge_grad, node_grad):
+    vmem = pl.BlockSpec(memory_space=pltpu.VMEM)
+    edge_part, node_part = pl.pallas_call(
+        reduce_kernel,
+        out_shape=(jax.ShapeDtypeStruct((12, 128), F32), jax.ShapeDtypeStruct((4, 128), F32)),
+        in_specs=[vmem, vmem],
+        out_specs=(vmem, vmem),
+        scratch_shapes=[
+            pltpu.VMEM((2, 1536, 128), F32),
+            pltpu.VMEM((2, 512, 128), F32),
+            pltpu.VMEM((3, 512, 256), BF),
+            pltpu.VMEM((3, 512, 256), BF),
+            pltpu.VMEM((512, 256), BF),
+            pltpu.VMEM((512, 256), BF),
+            pltpu.SemaphoreType.DMA((4,)),
+            pltpu.SemaphoreType.DMA((4,)),
+        ] + scatter_scratch(),
+        compiler_params=pltpu.CompilerParams(collective_id=0, has_side_effects=True, vmem_limit_bytes=40 * 1024 * 1024),
+        name="reduce_scatter",
+    )(edge_grad, node_grad)
+    return edge_part.reshape(-1), node_part.reshape(-1)
 
 
 def local(node_features, edge_features, open_faces, edge_weight, node_weight, cotangent):
@@ -69,7 +291,6 @@
     node_weight_grad = lax.dot_general(
         flat_summed, flat_update, (((0,), (0,)), ((), ())), preferred_element_type=jnp.float32
     )
-    node_flat = node_weight_grad.reshape(-1)
     grad_summed = lax.dot_general(
         flat_update, node_weight, (((1,), (1,)), ((), ())), preferred_element_type=jnp.float32
     )
@@ -104,11 +325,7 @@
     lower_second = passed_along(toward[1, :, -1:].astype(jnp.bfloat16), "gy", 1).astype(jnp.float32)
     node_grad = node_grad + jnp.concatenate([lower_first, toward[0, :-1]], axis=0)
     node_grad = node_grad + jnp.concatenate([lower_second, toward[1, :, :-1]], axis=1)
-    edge_flat = edge_weight_grad.reshape(-1)
-    edge_part, node_part = (
-        lax.psum_scatter(edge_flat, ("gx", "gy"), scatter_dimension=0, tiled=True),
-        lax.psum_scatter(node_flat, ("gx", "gy"), scatter_dimension=0, tiled=True),
-    )
+    edge_part, node_part = reduce_scatter(edge_weight_grad, node_weight_grad)
     return (new_nodes, node_grad.astype(jnp.bfloat16), edge_part, node_part)
 
 

time: 353 us -> 93.8 us (0.27)
  waiting for transfers between devices: 289 us -> 15.6 us
  Pallas kernels: 0 us -> 40.8 us
  between operations: 14.4 us -> 1 us
  starting transfers between devices: 27.5 us -> 21 us
  local copies, waits for them, and re-layouts: 11.2 us -> 4.81 us
    unnamed x2 -> x0, waiting for transfers between devices: 281 us -> none
    pallas_call x0 -> x1, Pallas kernels: none -> 40.8 us  [reduce_scatter(): pl.pallas_call(reduce_kernel, out_shape=(jax.ShapeDtypeStruct((12, 128),...]
    ppermute x8, waiting for transfers between devices: 7.8 us -> 15.6 us  [passed_along(): lax.ppermute(value, axis, [(source, source + steps) for source in range(f...]
    ppermute x8, starting transfers between devices: 27.4 us -> 21 us  [passed_along(): lax.ppermute(value, axis, [(source, source + steps) for source in range(f...]
    unnamed x12 -> x10, local copies, waits for them, and re-layouts: 7.55 us -> 1.2 us
  transfers between devices with their start and end apart: 9 -> 8, of which waited for: 5 -> 6; matrix products, arithmetic and copies ran while one was open for 2% -> 3% of each run, Pallas kernels for 0% -> 0%
where the time goes in v1:
time: 93.8 us; the launch traced here: 92.6 us
  Pallas kernels  40.8 us (43%)
  starting transfers between devices  21 us (22%)
  waiting for transfers between devices  15.6 us (17%)
  matrix products  5.99 us (6%)
  local copies, waits for them, and re-layouts  4.81 us (5%)
  other arithmetic  3.32 us (4%)
  between operations  1 us (1%)
    pallas_call x1, Pallas kernels, reduce_scatter(): pl.pallas_call(reduce_kernel, out_shape=(jax.ShapeDtypeStruct((12, 128),...  40.8 us
    ppermute x8, starting transfers between devices, passed_along(): lax.ppermute(value, axis, [(source, source + steps) for source in range(f...  21 us
    ppermute x8, waiting for transfers between devices, passed_along(): lax.ppermute(value, axis, [(source, source + steps) for source in range(f...  15.6 us
  transfers between devices with their start and end apart: 8, of which 6 were waited for; matrix products, arithmetic and copies ran while one was open for 3% of the time, Pallas kernels for 0%

profile of v1, /device:TPU:1, one launch (start us, length us, event | category | flops | bytes accessed | tf_op | source)
XLA Modules:
  0.0 92.6 jit_solution(10607494954649367002)
XLA Ops:
  0.6 0.0 copy-start
  0.6 0.0 copy-start.1
  0.7 1.1 %fusion.33 = (bf16[1,2,64,512]{3,2,1,0:T(8,128)(2,1)S(1)}, bf16[1,2,64,512]{3,2,1,0:T(8,128)(2,1)S(1)}) fusion(bf16[2,2,64,512]{3,2,1,0:T(8,128)(2,1)} %param.6), kind=kLoop, calls=%fused_computation.73 | loop fusion | bytes 524288 | tf_op jit(solution)/shard_map/slice | solution.py:258
  1.7 8.7 %collective-permute-start = (bf16[1,2,64,512]{3,2,1,0:T(8,128)(2,1)S(1)}, bf16[1,2,64,512]{3,2,1,0:T(8,128)(2,1)S(1)}, u32[]{:S(2)}, u32[]{:S(2)}) collective-permute-start(bf16[1,2,64,512]{3,2,1,0:T(8,128)(2,1)S(1)} %get-tuple-element.18), channel_id=1, source_target_pairs={{16,0},{32,16},{48,32},{64,48},{80,64},{96,80},{112,96},{128,112},... | collective-permute-start | bytes 393224 | tf_op jit(solution)/shard_map/ppermute | solution.py:12
  10.5 1.0 %fusion.34 = (bf16[2,1,64,512]{3,2,1,0:T(8,128)(2,1)S(1)}, bf16[2,1,64,512]{3,2,1,0:T(8,128)(2,1)S(1)}) fusion(bf16[2,2,64,512]{3,2,1,0:T(8,128)(2,1)} %param.6), kind=kLoop, calls=%fused_computation.74 | loop fusion | bytes 524288 | tf_op jit(solution)/shard_map/slice | solution.py:259
  11.5 1.3 %collective-permute-start.1 = (bf16[2,1,64,512]{3,2,1,0:T(8,128)(2,1)S(1)}, bf16[2,1,64,512]{3,2,1,0:T(8,128)(2,1)S(1)}, u32[]{:S(2)}, u32[]{:S(2)}) collective-permute-start(bf16[2,1,64,512]{3,2,1,0:T(8,128)(2,1)S(1)} %get-tuple-element.20), channel_id=1, source_target_pairs={{1,0},{2,1},{3,2},{4,3},{5,4},{6,5},{7,6},{8,7},{9,8},{10,9},{11,1... | collective-permute-start | bytes 393224 | tf_op jit(solution)/shard_map/ppermute | solution.py:12
  12.8 0.7 convert_element_type.98
  13.5 1.2 %slice_bitcast_fusion.11 = (bf16[2,2,64,512]{3,2,1,0:T(8,128)(2,1)S(1)}, bf16[2,2,64,512]{3,2,1,0:T(8,128)(2,1)S(1)}, bf16[2,2,64,512]{3,2,1,0:T(8,128)(2,1)S(1)}) fusion(bf16[3,2,2,64,512]{4,3,2,1,0:T(8,128)(2,1)} %param.7), kind=kLoop, calls=%fused_computation.55 | loop fusion | bytes 1572864 | tf_op jit(solution)/shard_map/squeeze | solution.py:264
  14.7 0.1 slice_multiply_fusion.2
  14.7 0.0 copy-done.1
  14.7 0.0 copy-start.2
  14.7 0.1 slice.117
  14.8 0.0 collective-permute-done
  14.8 3.7 %collective-permute-done.1 = bf16[2,1,64,512]{3,2,1,0:T(8,128)(2,1)S(1)} collective-permute-done((bf16[2,1,64,512]{3,2,1,0:T(8,128)(2,1)S(1)}, bf16[2,1,64,512]{3,2,1,0:T(8,128)(2,1)S(1)}, u32[]{:S(2)}, u32[]{:S(2)}) %collective-permute-start.1) | collective-permute-done | bytes 131104 | tf_op jit(solution)/shard_map/ppermute | solution.py:12
  18.6 0.3 fusion.6
  18.8 0.0 copy-done.2
  18.9 1.6 %fusion.30 = (f32[3,2,2,64,512]{4,3,2,1,0:T(8,128)S(1)}, bf16[3,2,2,64,512]{4,3,2,1,0:T(8,128)(2,1)S(1)}, f32[3,2,2,64,512]{4,3,2,1,0:T(8,128)S(1)}) fusion(f32[3,2,2,64]{3,2,1,0:T(2,128)S(1)} %pad_maximum_fusion, bf16[3,2,2,64,1536]{4,3,2,1,0:T(8,128)(2,1)S(1)} %bitcast.88, bf16[1536,512]{1,0:T(8,128)(2,1)S(1)} %copy-done.2), kind=kOutput, calls=%fused_computation.70 | convolution fusion | flops 1210712064 | bytes 7867392 | tf_op jit(solution)/shard_map/dot_general | solution.py:270
  20.6 1.4 %collective-permute-start.3 = (bf16[2,1,64,512]{3,2,0,1:T(8,128)(2,1)S(1)}, bf16[2,1,64,512]{3,2,0,1:T(8,128)(2,1)S(1)}, u32[]{:S(2)}, u32[]{:S(2)}) collective-permute-start(bf16[2,1,64,512]{3,2,0,1:T(8,128)(2,1)S(1)} %slice_bitcast_fusion.14), channel_id=1, source_target_pairs={{0,1},{1,2},{2,3},{3,4},{4,5},{5,6},{6,7},{7,8},{8,9},{9,10},{10,1... | collective-permute-start | bytes 393224 | tf_op jit(solution)/shard_map/ppermute | solution.py:12
  22.0 1.9 %collective-permute-start.2 = (bf16[1,2,64,512]{3,2,0,1:T(8,128)(2,1)S(1)}, bf16[1,2,64,512]{3,2,0,1:T(8,128)(2,1)S(1)}, u32[]{:S(2)}, u32[]{:S(2)}) collective-permute-start(bf16[1,2,64,512]{3,2,0,1:T(8,128)(2,1)S(1)} %slice_bitcast_fusion.15), channel_id=1, source_target_pairs={{0,16},{16,32},{32,48},{48,64},{64,80},{80,96},{96,112},{112,128},... | collective-permute-start | bytes 393224 | tf_op jit(solution)/shard_map/ppermute | solution.py:12
  23.9 0.7 collective-permute-done.3
  24.7 1.2 %collective-permute-done.2 = bf16[1,2,64,512]{3,2,0,1:T(8,128)(2,1)S(1)} collective-permute-done((bf16[1,2,64,512]{3,2,0,1:T(8,128)(2,1)S(1)}, bf16[1,2,64,512]{3,2,0,1:T(8,128)(2,1)S(1)}, u32[]{:S(2)}, u32[]{:S(2)}) %collective-permute-start.2) | collective-permute-done | bytes 131104 | tf_op jit(solution)/shard_map/ppermute | solution.py:12
  25.9 0.4 fusion.22
  26.2 0.0 copy-done
  26.3 0.0 copy-start.3
  26.3 1.1 %add_convert_fusion = (bf16[2,2,64,512]{3,2,1,0:T(8,128)(2,1)}, f32[2,2,64,512]{3,2,1,0:T(8,128)S(1)}) fusion(bf16[2,2,64,512]{3,2,1,0:T(8,128)(2,1)S(1)} %copy-done.1, bf16[512,512]{1,0:T(8,128)(2,1)S(1)} %copy-done, bf16[2,2,64,512]{3,2,0,1:T(8,128)(2,1)S(1)} %fusion.22), kind=kOutput, calls=%fused_computation.44 | convolution fusion | flops 135135232 | bytes 1835008 | tf_op jit(solution)/shard_map/dot_general | solution.py:285
  27.4 0.0 copy-done.3
  27.4 0.5 convolution_bitcast_fusion.node_in
  27.8 0.4 fusion.35
  28.3 1.9 %collective-permute-start.4 = (bf16[1,2,64,512]{3,2,1,0:T(8,128)(2,1)S(1)}, bf16[1,2,64,512]{3,2,1,0:T(8,128)(2,1)S(1)}, u32[]{:S(2)}, u32[]{:S(2)}) collective-permute-start(bf16[1,2,64,512]{3,2,1,0:T(8,128)(2,1)S(1)} %get-tuple-element.14), channel_id=1, source_target_pairs={{16,0},{32,16},{48,32},{64,48},{80,64},{96,80},{112,96},{128,112},... | collective-permute-start | bytes 393224 | tf_op jit(solution)/shard_map/ppermute | solution.py:12
  30.2 0.1 slice.159
  30.3 1.3 %collective-permute-start.5 = (bf16[2,1,64,512]{3,2,1,0:T(8,128)(2,1)S(1)}, bf16[2,1,64,512]{3,2,1,0:T(8,128)(2,1)S(1)}, u32[]{:S(2)}, u32[]{:S(2)}) collective-permute-start(bf16[2,1,64,512]{3,2,1,0:T(8,128)(2,1)S(1)} %get-tuple-element.16), channel_id=1, source_target_pairs={{1,0},{2,1},{3,2},{4,3},{5,4},{6,5},{7,6},{8,7},{9,8},{10,9},{11,1... | collective-permute-start | bytes 393224 | tf_op jit(solution)/shard_map/ppermute | solution.py:12
  31.6 3.9 %collective-permute-done.4 = bf16[1,2,64,512]{3,2,1,0:T(8,128)(2,1)S(1)} collective-permute-done((bf16[1,2,64,512]{3,2,1,0:T(8,128)(2,1)S(1)}, bf16[1,2,64,512]{3,2,1,0:T(8,128)(2,1)S(1)}, u32[]{:S(2)}, u32[]{:S(2)}) %collective-permute-start.4) | collective-permute-done | bytes 131104 | tf_op jit(solution)/shard_map/ppermute | solution.py:12
  35.6 2.0 %collective-permute-done.5 = bf16[2,1,64,512]{3,2,1,0:T(8,128)(2,1)S(1)} collective-permute-done((bf16[2,1,64,512]{3,2,1,0:T(8,128)(2,1)S(1)}, bf16[2,1,64,512]{3,2,1,0:T(8,128)(2,1)S(1)}, u32[]{:S(2)}, u32[]{:S(2)}) %collective-permute-start.5) | collective-permute-done | bytes 131104 | tf_op jit(solution)/shard_map/ppermute | solution.py:12
  37.6 0.7 multiply_convert_fusion
  38.3 1.0 %fusion.9 = f32[3,2,2,64,1024]{4,3,2,1,0:T(8,128)S(1)} fusion(bf16[3,2,2,64,512]{4,3,2,1,0:T(8,128)(2,1)S(1)} %multiply_convert_fusion, bf16[1536,512]{1,0:T(8,128)(2,1)S(1)} %copy-done.2), kind=kOutput, calls=%fused_computation.17 | convolution fusion | flops 805306368 | bytes 4980736 | tf_op jit(solution)/shard_map/dot_general | solution.py:313
  39.4 1.4 %fusion.36.edge_in = f32[1536,512]{1,0:T(8,128)S(1)} fusion(bf16[768,1536]{1,0:T(8,128)(2,1)S(1)} %bitcast.89, bf16[768,512]{1,0:T(8,128)(2,1)S(1)} %bitcast.87), kind=kOutput, calls=%fused_computation.76 | convolution fusion | flops 1207959552 | bytes 6291456 | tf_op jit(solution)/shard_map/dot_general | solution.py:310
  40.8 40.8 %reduce_scatter.1 = (f32[12,128]{1,0:T(8,128)S(1)}, f32[4,128]{1,0:T(4,128)S(1)}) custom-call(f32[1536,512]{1,0:T(8,128)S(1)} %fusion.36.edge_in, f32[512,512]{1,0:T(8,128)S(1)} %convolution_bitcast_fusion.node_in), custom_call_target="tpu_custom_call" | custom-call | tf_op jit(solution)/shard_map/reduce_scatter/pallas_call | solution.py:219
  81.7 2.5 %collective-permute-start.6 = (bf16[1,2,64,512]{3,2,1,0:T(8,128)(2,1)S(1)}, bf16[1,2,64,512]{3,2,1,0:T(8,128)(2,1)S(1)}, u32[]{:S(2)}, u32[]{:S(2)}) collective-permute-start(bf16[1,2,64,512]{3,2,1,0:T(8,128)(2,1)S(1)} %slice_bitcast_fusion.13), channel_id=1, source_target_pairs={{0,16},{16,32},{32,48},{48,64},{64,80},{80,96},{96,112},{112,128},... | collective-permute-start | bytes 393224 | tf_op jit(solution)/shard_map/ppermute | solution.py:12
  84.2 1.9 %collective-permute-start.7 = (bf16[2,1,64,512]{3,2,1,0:T(8,128)(2,1)S(1)}, bf16[2,1,64,512]{3,2,1,0:T(8,128)(2,1)S(1)}, u32[]{:S(2)}, u32[]{:S(2)}) collective-permute-start(bf16[2,1,64,512]{3,2,1,0:T(8,128)(2,1)S(1)} %slice_bitcast_fusion.12), channel_id=1, source_target_pairs={{0,1},{1,2},{2,3},{3,4},{4,5},{5,6},{6,7},{7,8},{8,9},{9,10},{10,1... | collective-permute-start | bytes 393224 | tf_op jit(solution)/shard_map/ppermute | solution.py:12
  86.2 0.0 collective-permute-done.6
  86.2 4.1 %collective-permute-done.7 = bf16[2,1,64,512]{3,2,1,0:T(8,128)(2,1)S(1)} collective-permute-done((bf16[2,1,64,512]{3,2,1,0:T(8,128)(2,1)S(1)}, bf16[2,1,64,512]{3,2,1,0:T(8,128)(2,1)S(1)}, u32[]{:S(2)}, u32[]{:S(2)}) %collective-permute-start.7) | collective-permute-done | bytes 131104 | tf_op jit(solution)/shard_map/ppermute | solution.py:12
  90.3 1.1 %fusion.18 = bf16[2,2,64,512]{3,2,1,0:T(8,128)(2,1)} fusion(bf16[2,2,64,512]{3,2,1,0:T(8,128)(2,1)S(1)} %copy-done.3, f32[3,2,2,64,1024]{4,3,2,1,0:T(8,128)S(1)} %fusion.9, f32[1,2,64,512]{3,2,1,0:T(8,128)S(1)} %slice_bitcast_fusion.6, f32[1,2,64,512]{3,2,1,0:T(8,128)S(1)} %convert_element_type.115, f32[2,1,64,512]{3,2,1,0:T(8,128)S(1)} %slice_bitcast_fusion.5, ...), kind=kLoop, calls=%fused_computation.28 | loop fusion | flops 1310720 | bytes 3661824 | tf_op jit(solution)/shard_map/convert_element_type | solution.py:329
  91.4 0.6 copy.36
  92.0 0.6 copy.37
  (22 shorter events, 0.4 us)
Async XLA Ops:
  0.6 25.6 %copy-start = (bf16[512,512]{1,0:T(8,128)(2,1)S(1)}, bf16[512,512]{1,0:T(8,128)(2,1)}, u32[]{:S(2)}) copy-start(bf16[512,512]{1,0:T(8,128)(2,1)} %param.10) | copy-start | bytes 1572868
  0.6 14.1 %copy-start.1 = (bf16[2,2,64,512]{3,2,1,0:T(8,128)(2,1)S(1)}, bf16[2,2,64,512]{3,2,1,0:T(8,128)(2,1)}, u32[]{:S(2)}) copy-start(bf16[2,2,64,512]{3,2,1,0:T(8,128)(2,1)} %param.6) | copy-start | bytes 786436
  1.7 13.1 %collective-permute-start = (bf16[1,2,64,512]{3,2,1,0:T(8,128)(2,1)S(1)}, bf16[1,2,64,512]{3,2,1,0:T(8,128)(2,1)S(1)}, u32[]{:S(2)}, u32[]{:S(2)}) collective-permute-start(bf16[1,2,64,512]{3,2,1,0:T(8,128)(2,1)S(1)} %get-tuple-element.18), channel_id=1, source_target_pairs={{16,0},{32,16},{48,32},{64,48},{80,64},{96,80},{112,96},{128,112},... | collective-permute-start | bytes 393224 | tf_op jit(solution)/shard_map/ppermute | solution.py:12
  11.5 7.1 %collective-permute-start.1 = (bf16[2,1,64,512]{3,2,1,0:T(8,128)(2,1)S(1)}, bf16[2,1,64,512]{3,2,1,0:T(8,128)(2,1)S(1)}, u32[]{:S(2)}, u32[]{:S(2)}) collective-permute-start(bf16[2,1,64,512]{3,2,1,0:T(8,128)(2,1)S(1)} %get-tuple-element.20), channel_id=1, source_target_pairs={{1,0},{2,1},{3,2},{4,3},{5,4},{6,5},{7,6},{8,7},{9,8},{10,9},{11,1... | collective-permute-start | bytes 393224 | tf_op jit(solution)/shard_map/ppermute | solution.py:12
  14.7 4.1 %copy-start.2 = (bf16[1536,512]{1,0:T(8,128)(2,1)S(1)}, bf16[1536,512]{1,0:T(8,128)(2,1)}, u32[]{:S(2)}) copy-start(bf16[1536,512]{1,0:T(8,128)(2,1)} %param.9) | copy-start | bytes 4718596
  20.6 4.1 %collective-permute-start.3 = (bf16[2,1,64,512]{3,2,0,1:T(8,128)(2,1)S(1)}, bf16[2,1,64,512]{3,2,0,1:T(8,128)(2,1)S(1)}, u32[]{:S(2)}, u32[]{:S(2)}) collective-permute-start(bf16[2,1,64,512]{3,2,0,1:T(8,128)(2,1)S(1)} %slice_bitcast_fusion.14), channel_id=1, source_target_pairs={{0,1},{1,2},{2,3},{3,4},{4,5},{5,6},{6,7},{7,8},{8,9},{9,10},{10,1... | collective-permute-start | bytes 393224 | tf_op jit(solution)/shard_map/ppermute | solution.py:12
  22.0 3.9 %collective-permute-start.2 = (bf16[1,2,64,512]{3,2,0,1:T(8,128)(2,1)S(1)}, bf16[1,2,64,512]{3,2,0,1:T(8,128)(2,1)S(1)}, u32[]{:S(2)}, u32[]{:S(2)}) collective-permute-start(bf16[1,2,64,512]{3,2,0,1:T(8,128)(2,1)S(1)} %slice_bitcast_fusion.15), channel_id=1, source_target_pairs={{0,16},{16,32},{32,48},{48,64},{64,80},{80,96},{96,112},{112,128},... | collective-permute-start | bytes 393224 | tf_op jit(solution)/shard_map/ppermute | solution.py:12
  26.3 1.1 %copy-start.3 = (bf16[2,2,64,512]{3,2,1,0:T(8,128)(2,1)S(1)}, bf16[2,2,64,512]{3,2,1,0:T(8,128)(2,1)}, u32[]{:S(2)}) copy-start(bf16[2,2,64,512]{3,2,1,0:T(8,128)(2,1)} %param.11) | copy-start | bytes 786436
  28.3 7.3 %collective-permute-start.4 = (bf16[1,2,64,512]{3,2,1,0:T(8,128)(2,1)S(1)}, bf16[1,2,64,512]{3,2,1,0:T(8,128)(2,1)S(1)}, u32[]{:S(2)}, u32[]{:S(2)}) collective-permute-start(bf16[1,2,64,512]{3,2,1,0:T(8,128)(2,1)S(1)} %get-tuple-element.14), channel_id=1, source_target_pairs={{16,0},{32,16},{48,32},{64,48},{80,64},{96,80},{112,96},{128,112},... | collective-permute-start | bytes 393224 | tf_op jit(solution)/shard_map/ppermute | solution.py:12
  30.3 7.3 %collective-permute-start.5 = (bf16[2,1,64,512]{3,2,1,0:T(8,128)(2,1)S(1)}, bf16[2,1,64,512]{3,2,1,0:T(8,128)(2,1)S(1)}, u32[]{:S(2)}, u32[]{:S(2)}) collective-permute-start(bf16[2,1,64,512]{3,2,1,0:T(8,128)(2,1)S(1)} %get-tuple-element.16), channel_id=1, source_target_pairs={{1,0},{2,1},{3,2},{4,3},{5,4},{6,5},{7,6},{8,7},{9,8},{10,9},{11,1... | collective-permute-start | bytes 393224 | tf_op jit(solution)/shard_map/ppermute | solution.py:12
  81.7 4.5 %collective-permute-start.6 = (bf16[1,2,64,512]{3,2,1,0:T(8,128)(2,1)S(1)}, bf16[1,2,64,512]{3,2,1,0:T(8,128)(2,1)S(1)}, u32[]{:S(2)}, u32[]{:S(2)}) collective-permute-start(bf16[1,2,64,512]{3,2,1,0:T(8,128)(2,1)S(1)} %slice_bitcast_fusion.13), channel_id=1, source_target_pairs={{0,16},{16,32},{32,48},{48,64},{64,80},{80,96},{96,112},{112,128},... | collective-permute-start | bytes 393224 | tf_op jit(solution)/shard_map/ppermute | solution.py:12
  84.2 6.1 %collective-permute-start.7 = (bf16[2,1,64,512]{3,2,1,0:T(8,128)(2,1)S(1)}, bf16[2,1,64,512]{3,2,1,0:T(8,128)(2,1)S(1)}, u32[]{:S(2)}, u32[]{:S(2)}) collective-permute-start(bf16[2,1,64,512]{3,2,1,0:T(8,128)(2,1)S(1)} %slice_bitcast_fusion.12), channel_id=1, source_target_pairs={{0,1},{1,2},{2,3},{3,4},{4,5},{5,6},{6,7},{7,8},{8,9},{9,10},{10,1... | collective-permute-start | bytes 393224 | tf_op jit(solution)/shard_map/ppermute | solution.py:12

commit v2 on v1

v2 whole, which is shorter than its diff:
```python
import jax
import jax.numpy as jnp
from jax import lax
from jax.experimental import pallas as pl
from jax.experimental.pallas import tpu as pltpu
from jax.sharding import PartitionSpec as P

MESH = pl.DeviceIdType.MESH
BF = jnp.bfloat16
F32 = jnp.float32


class Place:
    def __init__(self):
        gx, gy = lax.axis_index("gx"), lax.axis_index("gy")
        self.gx, self.gy = gx, gy
        self.x_hi, self.y, self.core = gx // 16, (gx // 2) % 8, gx % 2
        self.z, self.x_lo = gy // 2, gy % 2
        self.x = self.x_hi * 2 + self.x_lo
        self.sibling = (gx + 1 - 2 * self.core, gy)

    def along(self, axis, step):
        if axis == "x":
            other = (self.x + step) % 4
            return other, ((other // 2) * 16 + self.y * 2 + self.core, self.z * 2 + other % 2)
        if axis == "y":
            other = (self.y + step) % 8
            return other, (self.x_hi * 16 + other * 2 + self.core, self.gy)
        other = (self.z + step) % 8
        return other, (self.gx, other * 2 + self.x_lo)

    def beside(self, first, second):
        return ((self.gx + first) % 32, (self.gy + second) % 16)

    def partners(self):
        found = [self.sibling, self.beside(1, 0), self.beside(-1, 0), self.beside(0, 1), self.beside(0, -1)]
        for axis, count in (("x", 4), ("y", 8), ("z", 8)):
            found += [self.along(axis, step)[1] for step in range(1, count)]
        return found


def greet(devices, meanwhile):
    barrier = pltpu.get_barrier_semaphore()
    for device in devices:
        pl.semaphore_signal(barrier, inc=1, device_id=device, device_id_type=MESH)
    meanwhile()
    pl.semaphore_wait(barrier, len(devices))


def push(source, target, send_sem, recv_sem, device):
    copy = pltpu.make_async_remote_copy(
        src_ref=source, dst_ref=target, send_sem=send_sem, recv_sem=recv_sem, device_id=device, device_id_type=MESH
    )
    copy.start()
    return copy


SIZES = {"x": 4, "y": 8, "z": 8}
FAR = {4: (2, 1, 3), 8: (4, 3, 5, 2, 6, 1, 7)}
ORDERS = (("x", "y", "z"), ("y", "x", "z"), ("z", "x", "y"), ("x", "z", "y"))
TYPES = {0: (0, 0), 1: (0, 1), 3: (1, 0), 2: (1, 1)}


def scatter_scratch():
    shapes = []
    for first, second, _ in ORDERS:
        one, two = SIZES[first], SIZES[second]
        shapes += [pltpu.VMEM((one, 2, two, 16, 128), BF)] * 2
        shapes += [pltpu.VMEM((two, 2, 16, 128), BF)] * 2
    shapes += [pltpu.VMEM((2, 64, 128), F32)]
    shapes += [pltpu.VMEM((2, 8, 8, 128), F32)] * 2
    shapes += [pltpu.VMEM((2, 8, 128), F32)] * 2
    shapes += [pltpu.SemaphoreType.DMA((4, 8))] * 4 + [pltpu.SemaphoreType.DMA((2, 8))] * 2
    shapes += [pltpu.SemaphoreType.DMA] * 2
    return shapes


def fill_first(place, plane, step, edge, node, out):
    first, second, _ = ORDERS[plane]
    dest, device = place.along(first, step)
    for c in range(2):
        if plane == 0:
            start = 768 * (dest // 2) + 3 * (dest % 2)
            rows = edge[c, pl.ds(start, 128, stride=6), :]
            out[step, c] = rows.astype(BF).reshape(8, 16, 128)
        elif plane == 1:
            for hi in range(2):
                for lo in range(2):
                    start = 768 * hi + 3 * lo + 1 + 96 * dest
                    out[step, c, 2 * hi + lo] = edge[c, pl.ds(start, 16, stride=6), :].astype(BF)
        elif plane == 2:
            for hi in range(2):
                for lo in range(2):
                    start = 768 * hi + 3 * lo + 2 + 6 * dest
                    rows = [edge[c, pl.ds(start + 48 * core, 8, stride=96), :] for core in range(2)]
                    out[step, c, 2 * hi + lo] = jnp.concatenate(rows, axis=0).astype(BF)
        else:
            for high in range(8):
                start = 256 * (dest // 2) + dest % 2 + 2 * high
                rows = [node[c, pl.ds(start + 16 * core, 8, stride=32), :] for core in range(2)]
                out[step, c, high] = jnp.concatenate(rows, axis=0).astype(BF)
    return device


def scatter(place, edge, node, scratch, meanwhile, planes_first=(1, 2, 0, 3)):
    bufs = [scratch[4 * plane: 4 * plane + 4] for plane in range(4)]
    wide, send_three, recv_three, last, last_in = scratch[16:21]
    send_1, recv_1, send_2, recv_2, send_3, recv_3, send_4, recv_4 = scratch[21:29]
    stage_1 = {plane: {} for plane in range(4)}
    stage_2 = {plane: {} for plane in range(4)}
    for plane in planes_first:
        first = ORDERS[plane][0]
        out, landing = bufs[plane][:2]
        for step in FAR[SIZES[first]]:
            device = fill_first(place, plane, step, edge, node, out)
            stage_1[plane][step] = push(out.at[step], landing.at[step], send_1.at[plane, step], recv_1.at[plane, step], device)
        fill_first(place, plane, 0, edge, node, out)
    meanwhile()
    for plane in planes_first:
        first, second, _ = ORDERS[plane]
        out, landing, out_2, landing_2 = bufs[plane]
        for step in (1, 7, 2, 6, 3, 5, 4) if SIZES[first] == 8 else (1, 3, 2):
            stage_1[plane][step].wait_recv()
        for step in FAR[SIZES[second]] + (0,):
            dest, device = place.along(second, step)
            total = out[0, :, dest].astype(F32)
            for source in range(1, SIZES[first]):
                total = total + landing[source, :, dest].astype(F32)
            out_2[step] = total.astype(BF)
            if step:
                stage_2[plane][step] = push(out_2.at[step], landing_2.at[step], send_2.at[plane, step], recv_2.at[plane, step], device)
    stage_3 = []
    for kind, axis in ((0, "z"), (1, "y")):
        for plane in range(4):
            if TYPES[plane][0] != kind:
                continue
            out_2, landing_2 = bufs[plane][2:]
            count = SIZES[ORDERS[plane][1]]
            for step in range(1, count):
                stage_2[plane][step].wait_recv()
            total = out_2[0].astype(F32)
            for source in range(1, count):
                total = total + landing_2[source].astype(F32)
            slot = TYPES[plane][1]
            for c in range(2):
                for core in range(2):
                    row = (core * 4 + slot * 2 + c) * 8
                    wide[kind, pl.ds(row, 8), :] = total[c, core * 8: core * 8 + 8]
        for step in FAR[8] + (0,):
            dest, device = place.along(axis, step)
            send_three[kind, step] = wide[kind, pl.ds(dest, 8, stride=8), :]
            if step:
                stage_3.append(push(send_three.at[kind, step], recv_three.at[kind, step], send_3.at[kind, step], recv_3.at[kind, step], device))
    for copy in stage_3:
        copy.wait_recv()
    for kind in range(2):
        total = send_three[kind, 0]
        for step in range(1, 8):
            total = total + recv_three[kind, step]
        last[kind] = total
    swap = push(last, last_in, send_4, recv_4, place.sibling)
    swap.wait_recv()
    pending = stage_3 + [swap]
    for plane in range(4):
        pending += list(stage_1[plane].values()) + list(stage_2[plane].values())

    def finish(edge_out, node_out):
        for plane in range(4):
            kind, slot = TYPES[plane]
            rows = pl.ds(place.core * 4 + slot * 2, 2)
            mine, theirs = last[kind, rows, :], last_in[kind, rows, :]
            low = jnp.where(place.core == 0, mine, theirs)
            high = jnp.where(place.core == 0, theirs, mine)
            if plane < 3:
                edge_out[pl.ds(4 * plane, 2), :] = low
                edge_out[pl.ds(4 * plane + 2, 2), :] = high
            else:
                node_out[pl.ds(0, 2), :] = low
                node_out[pl.ds(2, 2), :] = high
        for copy in pending:
            copy.wait_send()

    return finish


def mul(left, right):
    return jnp.dot(left, right, preferred_element_type=F32)


def mul_nt(left, right):
    return lax.dot_general(left, right, (((1,), (1,)), ((), ())), preferred_element_type=F32)


def mul_tn(left, right):
    return lax.dot_general(left, right, (((0,), (0,)), ((), ())), preferred_element_type=F32)


def sigmoid(value):
    return 0.5 + 0.5 * jnp.tanh(0.5 * value)


BLOCKS = ((0, 0), (0, 1), (1, 0), (1, 1))


def step_kernel(nf_in, ef_in, faces_in, we_in, wn_in, cot_in, nn_out, ng_out, edge_out, node_out,
                nf, ef, faces, we, wn, cot, spread, masks, pre, self_part, upper_part,
                halo_x, halo_y, msg, in_x, in_y, summed, gu, gs, gs_x, gs_y, gp, gp_x, gp_y, gsum, tsum,
                nf_t, hx_t, hy_t, ef_t, nn, ng, load_sem, store_sem, halo_send, halo_recv,
                edge, node, edge_to, edge_from, node_to, node_from, swap_send, swap_recv, *scratch):
    place = Place()
    mine = pl.multiple_of(place.core * 256, 256)
    other = pl.multiple_of(256 - place.core * 256, 256)
    loads = []

    def load():
        for index, (source, target) in enumerate(((nf_in, nf), (we_in, we), (ef_in, ef), (faces_in, faces), (wn_in, wn), (cot_in, cot))):
            copy = pltpu.make_async_copy(source, target, load_sem.at[index])
            copy.start()
            loads.append(copy)

    greet(place.partners(), load)
    down_x, up_x = place.beside(-1, 0), place.beside(1, 0)
    down_y, up_y = place.beside(0, -1), place.beside(0, 1)
    halos = {}

    def trade(index, source, target, device):
        halos[index] = push(source, target, halo_send.at[index], halo_recv.at[index], device)

    trade(1, nf_in.at[:, 0], halo_y, down_y)
    trade(0, nf_in.at[0], halo_x, down_x)

    loads[3].wait()
    spread[...] = jnp.zeros_like(spread)
    inside_x = jnp.where(place.gx < 31, 1.0, 0.0)
    inside_y = jnp.where(place.gy < 15, 1.0, 0.0)
    depth = lax.broadcasted_iota(jnp.int32, (2, 64), 1)
    second = lax.broadcasted_iota(jnp.int32, (2, 64), 0)
    for a in range(2):
        rows = faces[0, a].astype(F32)
        spread[pl.ds(2 * a, 2), :] = rows * inside_x if a else rows
        rows = faces[1, a].astype(F32)
        spread[pl.ds(4 + 2 * a, 2), :] = jnp.where(second == 1, rows * inside_y, rows)
        rows = faces[2, a].astype(F32)
        spread[pl.ds(8 + 2 * a, 2), :] = jnp.where(depth < 63, rows, 0.0)
    eye = lax.broadcasted_iota(jnp.int32, (64, 64), 0) == lax.broadcasted_iota(jnp.int32, (64, 64), 1)
    for row in range(12):
        column = jnp.where(eye, jnp.broadcast_to(spread[pl.ds(row, 1), :], (64, 64)), 0.0)
        masks[row] = jnp.broadcast_to(jnp.sum(column, axis=1, keepdims=True), (64, 128))

    loads[0].wait()
    loads[1].wait()
    own = nf[...].reshape(256, 512)
    self_part[...] = mul(own, we[0:512, :]).reshape(2, 2, 64, 512)
    upper_part[...] = mul(own, we[512:1024, :]).reshape(2, 2, 64, 512)
    loads[2].wait()
    for d in (2, 1, 0):
        stored = mul(ef[d].reshape(256, 512), we[1024:1536, :]).reshape(2, 2, 64, 512)
        pre[d] = stored + self_part[...]

    def edge_block(d, a, b, upper):
        mask = jnp.concatenate([masks[4 * d + 2 * a + b]] * 4, axis=1)
        value = pre[d, a, b] + upper
        s = sigmoid(value)
        msg[d, a, b] = (value * s * mask).astype(BF)
        pre[d, a, b] = mask * (s * (1.0 + value * (1.0 - s)))

    @pl.loop(0, 2)
    def _(a):
        for b in range(2):
            edge_block(2, a, b, pltpu.roll(upper_part[a, b], 63, 0))
        edge_block(0, 0, a, upper_part[1, a])
        edge_block(1, a, 0, upper_part[a, 1])

    nf_t[...] = own.T

    halos[1].wait_recv()
    self_part[0] = mul(halo_y[...].reshape(128, 512), we[512:1024, :]).reshape(2, 64, 512)
    @pl.loop(0, 2)
    def _(a):
        edge_block(1, a, 1, self_part[0, a])

    trade(3, msg.at[1, :, 1], in_y, up_y)
    halos[0].wait_recv()
    self_part[1] = mul(halo_x[...].reshape(128, 512), we[512:1024, :]).reshape(2, 64, 512)
    @pl.loop(0, 2)
    def _(b):
        edge_block(0, 1, b, self_part[1, b])

    trade(2, msg.at[0, 1], in_x, up_x)

    for d in range(3):
        ef_t[:, 256 * d: 256 * d + 256] = ef[d].reshape(256, 512).T
    hx_t[...] = halo_x[...].reshape(128, 512).T
    hy_t[...] = halo_y[...].reshape(128, 512).T
    loads[4].wait()
    loads[5].wait()

    halos[3].wait_recv()
    halos[2].wait_recv()
    for a, b in BLOCKS:
        third = msg[2, a, b].astype(F32)
        total = msg[0, a, b].astype(F32) + msg[1, a, b].astype(F32) + third
        total = total - pltpu.roll(third, 1, 0)
        total = total - (in_x[b] if a == 0 else msg[0, 0, b]).astype(F32)
        total = total - (in_y[a] if b == 0 else msg[1, a, 0]).astype(F32)
        summed[pl.ds(128 * a + 64 * b, 64), :] = total.astype(BF)
    upper_part[...] = mul(summed[...], wn[...]).reshape(2, 2, 64, 512)
    @pl.loop(0, 4)
    def _(block):
        a, b = block // 2, block % 2
        value = upper_part[a, b]
        s = sigmoid(value)
        nn[a, b] = (nf[a, b].astype(F32) + value * s).astype(BF)
        rows = pl.ds(pl.multiple_of(64 * block, 64), 64)
        gu[rows, :] = (cot[a, b].astype(F32) * (s * (1.0 + value * (1.0 - s)))).astype(BF)

    gs[...] = mul_nt(gu[...], wn[...]).astype(BF).reshape(2, 2, 64, 512)
    trade(5, gs.at[:, 0], gs_y, down_y)
    trade(4, gs.at[0], gs_x, down_x)
    store_nn = pltpu.make_async_copy(nn, nn_out, store_sem.at[0])
    store_nn.start()

    node_to[...] = mul_tn(summed[...], gu[:, pl.ds(other, 256)]).astype(BF)
    swaps = [push(node_to, node_from, swap_send.at[3], swap_recv.at[3], place.sibling)]
    for c in range(2):
        node[c] = mul_tn(summed[...], gu[:, pl.ds(pl.multiple_of(mine + 128 * c, 128), 128)])

    def grad_block(d, a, b, above):
        gp[d, a, b] = ((gs[a, b].astype(F32) - above) * pre[d, a, b]).astype(BF)

    for a, b in BLOCKS:
        grad_block(2, a, b, pltpu.roll(gs[a, b].astype(F32), 63, 0))
    for b in range(2):
        grad_block(0, 0, b, gs[1, b].astype(F32))
    for a in range(2):
        grad_block(1, a, 0, gs[a, 1].astype(F32))
    swaps[0].wait_recv()
    for c in range(2):
        node[c] = node[c] + node_from[:, 128 * c: 128 * c + 128].astype(F32)
    halos[5].wait_recv()
    for a in range(2):
        grad_block(1, a, 1, gs_y[a].astype(F32))
    trade(7, gp.at[1, :, 1], gp_y, up_y)
    halos[4].wait_recv()
    for b in range(2):
        grad_block(0, 1, b, gs_x[b].astype(F32))
    trade(6, gp.at[0, 1], gp_x, up_x)
    for a, b in BLOCKS:
        rows = pl.ds(128 * a + 64 * b, 64)
        third = gp[2, a, b].astype(F32)
        gsum[rows, :] = (gp[0, a, b].astype(F32) + gp[1, a, b].astype(F32) + third).astype(BF)
        total = pltpu.roll(third, 1, 0)
        if a:
            total = total + gp[0, 0, b].astype(F32)
        if b:
            total = total + gp[1, a, 0].astype(F32)
        tsum[rows, :] = total.astype(BF)

    def grads(part, columns):
        if part == 0:
            return mul(nf_t[...], gsum[:, columns])
        if part == 1:
            total = mul(nf_t[...], tsum[:, columns])
            total = total + mul(hx_t[...], gp[0, 1, :, :, columns].reshape(128, 256))
            return total + mul(hy_t[...], gp[1, :, 1, :, columns].reshape(128, 256))
        return mul(ef_t[...], gp[:, :, :, :, columns].reshape(768, 256))

    for part in range(3):
        edge_to[part] = grads(part, pl.ds(other, 256)).astype(BF)
        swaps.append(push(edge_to.at[part], edge_from.at[part], swap_send.at[part], swap_recv.at[part], place.sibling))
    for part in range(3):
        total = grads(part, pl.ds(mine, 256))
        for c in range(2):
            edge[c, pl.ds(512 * part, 512), :] = total[:, 128 * c: 128 * c + 128]
    for part in range(3):
        swaps[part + 1].wait_recv()
        for c in range(2):
            rows = pl.ds(512 * part, 512)
            edge[c, rows, :] = edge[c, rows, :] + edge_from[part, :, 128 * c: 128 * c + 128].astype(F32)

    def node_grads():
        halos[6].wait_recv()
        halos[7].wait_recv()
        for a, b in BLOCKS:
            total = pltpu.roll(gp[2, a, b].astype(F32), 1, 0)
            total = total + (gp[0, 0, b] if a else gp_x[b]).astype(F32)
            total = total + (gp[1, a, 0] if b else gp_y[a]).astype(F32)
            tsum[pl.ds(128 * a + 64 * b, 64), :] = total.astype(BF)
        upper_part[...] = (mul_nt(gsum[...], we[0:512, :]) + mul_nt(tsum[...], we[512:1024, :])).reshape(2, 2, 64, 512)

        @pl.loop(0, 4)
        def _(block):
            a, b = block // 2, block % 2
            ng[a, b] = (cot[a, b].astype(F32) + upper_part[a, b]).astype(BF)

        pltpu.make_async_copy(ng, ng_out, store_sem.at[1]).start()

    finish = scatter(place, edge, node, scratch, node_grads)
    finish(edge_out, node_out)
    for copy in swaps + list(halos.values()):
        copy.wait_send()
    store_nn.wait()
    pltpu.make_async_copy(ng, ng_out, store_sem.at[1]).wait()


def local(node_features, edge_features, open_faces, edge_weight, node_weight, cotangent):
    anywhere = pl.BlockSpec(memory_space=pltpu.HBM)
    vmem = pl.BlockSpec(memory_space=pltpu.VMEM)
    nodes = (2, 2, 64, 512)
    plane = (2, 64, 512)
    new_nodes, node_grad, edge_part, node_part = pl.pallas_call(
        step_kernel,
        out_shape=(
            jax.ShapeDtypeStruct(nodes, BF),
            jax.ShapeDtypeStruct(nodes, BF),
            jax.ShapeDtypeStruct((12, 128), F32),
            jax.ShapeDtypeStruct((4, 128), F32),
        ),
        in_specs=[anywhere] * 6,
        out_specs=(anywhere, anywhere, vmem, vmem),
        scratch_shapes=[
            pltpu.VMEM(nodes, BF),
            pltpu.VMEM((3,) + nodes, BF),
            pltpu.VMEM((3, 2, 2, 64), jnp.int32),
            pltpu.VMEM((1536, 512), BF),
            pltpu.VMEM((512, 512), BF),
            pltpu.VMEM(nodes, BF),
            pltpu.VMEM((16, 64), F32),
            pltpu.VMEM((12, 64, 128), F32),
            pltpu.VMEM((3,) + nodes, F32),
            pltpu.VMEM(nodes, F32),
            pltpu.VMEM(nodes, F32),
            pltpu.VMEM(plane, BF),
            pltpu.VMEM(plane, BF),
            pltpu.VMEM((3,) + nodes, BF),
            pltpu.VMEM(plane, BF),
            pltpu.VMEM(plane, BF),
            pltpu.VMEM((256, 512), BF),
            pltpu.VMEM((256, 512), BF),
            pltpu.VMEM(nodes, BF),
            pltpu.VMEM(plane, BF),
            pltpu.VMEM(plane, BF),
            pltpu.VMEM((3,) + nodes, BF),
            pltpu.VMEM(plane, BF),
            pltpu.VMEM(plane, BF),
            pltpu.VMEM((256, 512), BF),
            pltpu.VMEM((256, 512), BF),
            pltpu.VMEM((512, 256), BF),
            pltpu.VMEM((512, 128), BF),
            pltpu.VMEM((512, 128), BF),
            pltpu.VMEM((512, 768), BF),
            pltpu.VMEM(nodes, BF),
            pltpu.VMEM(nodes, BF),
            pltpu.SemaphoreType.DMA((6,)),
            pltpu.SemaphoreType.DMA((2,)),
            pltpu.SemaphoreType.DMA((8,)),
            pltpu.SemaphoreType.DMA((8,)),
            pltpu.VMEM((2, 1536, 128), F32),
            pltpu.VMEM((2, 512, 128), F32),
            pltpu.VMEM((3, 512, 256), BF),
            pltpu.VMEM((3, 512, 256), BF),
            pltpu.VMEM((512, 256), BF),
            pltpu.VMEM((512, 256), BF),
            pltpu.SemaphoreType.DMA((4,)),
            pltpu.SemaphoreType.DMA((4,)),
        ] + scatter_scratch(),
        compiler_params=pltpu.CompilerParams(collective_id=0, has_side_effects=True, vmem_limit_bytes=64000000),
        name="mesh_step",
    )(node_features, edge_features, open_faces, edge_weight, node_weight, cotangent)
    return new_nodes, node_grad, edge_part.reshape(-1), node_part.reshape(-1)


def solution(mesh):
    placed = (
        P("gx", "gy", None, None),
        P(None, "gx", "gy", None, None),
        P(None, "gx", "gy", None),
        P(),
        P(),
        P("gx", "gy", None, None),
    )
    return jax.shard_map(
        local,
        mesh=mesh,
        in_specs=placed,
        out_specs=(
            P("gx", "gy", None, None),
            P("gx", "gy", None, None),
            P(("gx", "gy")),
            P(("gx", "gy")),
        ),
        check_vma=False,
    )
```

time: 93.8 us -> 64.9 us (0.69)
  starting transfers between devices: 21 us -> 0 us
  Pallas kernels: 40.8 us -> 58.1 us
  waiting for transfers between devices: 15.6 us -> 0 us
  matrix products: 5.99 us -> 0 us
  other arithmetic: 3.32 us -> 0 us
  local copies, waits for them, and re-layouts: 4.81 us -> 5.88 us
    ppermute x8 -> x0, starting transfers between devices: 21 us -> none  [passed_along(): lax.ppermute(value, axis, [(source, source + steps) for source in range(f...]
    pallas_call x1, Pallas kernels: 40.8 us -> 58.1 us  [local(): pl.pallas_call(step_kernel, out_shape=(jax.ShapeDtypeStruct(nodes, BF), j...]
    ppermute x8 -> x0, waiting for transfers between devices: 15.6 us -> none  [passed_along(): lax.ppermute(value, axis, [(source, source + steps) for source in range(f...]
    dot_general x6 -> x0, matrix products: 5.99 us -> none  [the longest x1 1.6 us: local(): jnp.dot(flat_inputs, edge_weight, preferred_element_type=jnp.float32)]
    unnamed x10 -> x4, local copies, waits for them, and re-layouts: 1.2 us -> 5.88 us
    convert_element_type x10 -> x0, other arithmetic: 2.92 us -> none  [the longest x1 1.1 us: local(): return (new_nodes, node_grad.astype(jnp.bfloat16), edge_part, node_part)]
    slice x6 -> x0, local copies, waits for them, and re-layouts: 2.22 us -> none  [the longest x1 1.06 us: local(): node_features[1:]]
    squeeze x9 -> x0, local copies, waits for them, and re-layouts: 1.33 us -> none  [the longest x1 1.16 us: local(): edge_features[direction]]
  transfers between devices with their start and end apart: 8 -> 0, of which waited for: 6 -> 0; matrix products, arithmetic and copies ran while one was open for 3% -> 0% of each run, Pallas kernels for 0% -> 0%
where the time goes in v2:
time: 64.9 us; the launch traced here: 64.6 us
  Pallas kernels  58.1 us (90%)
  local copies, waits for them, and re-layouts  5.88 us (9%)
    pallas_call x1, Pallas kernels, local(): pl.pallas_call(step_kernel, out_shape=(jax.ShapeDtypeStruct(nodes, BF), j...  58.1 us
    unnamed x4, local copies, waits for them, and re-layouts  5.88 us

profile of v2, /device:TPU:1, one launch (start us, length us, event | category | flops | bytes accessed | tf_op | source)
XLA Modules:
  0.0 64.6 jit_solution(8538460371409128811)
XLA Ops:
  0.6 58.1 %mesh_step.1 = (bf16[2,2,64,512]{3,2,1,0:T(8,128)(2,1)}, bf16[2,2,64,512]{3,2,1,0:T(8,128)(2,1)}, f32[12,128]{1,0:T(8,128)}, f32[4,128]{1,0:T(4,128)}) custom-call(bf16[2,2,64,512]{3,2,1,0:T(8,128)(2,1)} %nf_in.1, bf16[3,2,2,64,512]{4,3,2,1,0:T(8,128)(2,1)} %ef_in.1, s32[3,2,2,64]{3,2,1,0:T(2,128)} %faces_in.1, bf16[1536,512]{1,0:T(8,128)(2,1)} %we_in.1, ...), custom_call_target="tpu_custom_call" | custom-call | tf_op jit(solution)/shard_map/mesh_step/pallas_call | solution.py:411
  58.7 1.7 %copy.14 = bf16[2,2,64,512]{3,2,1,0:T(8,128)(2,1)} copy(bf16[2,2,64,512]{3,2,1,0:T(8,128)(2,1)} %get-tuple-element.16) | data formatting | bytes 524288
  60.4 1.7 %copy.15 = bf16[2,2,64,512]{3,2,1,0:T(8,128)(2,1)} copy(bf16[2,2,64,512]{3,2,1,0:T(8,128)(2,1)} %get-tuple-element.17) | data formatting | bytes 524288
  62.1 1.3 %copy.16 = f32[1536]{0:T(1024)} copy(f32[1536]{0:T(1024)} %bitcast.2) | data formatting | bytes 12288
  63.4 1.2 %copy.17 = f32[512]{0:T(512)} copy(f32[512]{0:T(512)} %bitcast.3) | data formatting | bytes 4096

commit v3 on v2

--- a/solution.py
+++ b/solution.py
@@ -204,7 +204,7 @@
 
 def step_kernel(nf_in, ef_in, faces_in, we_in, wn_in, cot_in, nn_out, ng_out, edge_out, node_out,
                 nf, ef, faces, we, wn, cot, spread, masks, pre, self_part, upper_part,
-                halo_x, halo_y, msg, in_x, in_y, summed, gu, gs, gs_x, gs_y, gp, gp_x, gp_y, gsum, tsum,
+                halo, update, msg, in_x, in_y, summed, gu, gs, gs_x, gs_y, gp, gp_x, gp_y, gsum, tsum,
                 nf_t, hx_t, hy_t, ef_t, nn, ng, load_sem, store_sem, halo_send, halo_recv,
                 edge, node, edge_to, edge_from, node_to, node_from, swap_send, swap_recv, *scratch):
     place = Place()
@@ -226,8 +226,9 @@
     def trade(index, source, target, device):
         halos[index] = push(source, target, halo_send.at[index], halo_recv.at[index], device)
 
-    trade(1, nf_in.at[:, 0], halo_y, down_y)
-    trade(0, nf_in.at[0], halo_x, down_x)
+    for c in (1, 0):
+        trade(2 + c, nf_in.at[pl.ds(128 * c, 64)], halo.at[c, 1], down_y)
+        trade(c, nf_in.at[pl.ds(64 * c, 64)], halo.at[c, 0], down_x)
 
     loads[3].wait()
     spread[...] = jnp.zeros_like(spread)
@@ -249,7 +250,7 @@
 
     loads[0].wait()
     loads[1].wait()
-    own = nf[...].reshape(256, 512)
+    own = nf[...]
     self_part[...] = mul(own, we[0:512, :]).reshape(2, 2, 64, 512)
     upper_part[...] = mul(own, we[512:1024, :]).reshape(2, 2, 64, 512)
     loads[2].wait()
@@ -273,50 +274,60 @@
 
     nf_t[...] = own.T
 
-    halos[1].wait_recv()
-    self_part[0] = mul(halo_y[...].reshape(128, 512), we[512:1024, :]).reshape(2, 64, 512)
-    @pl.loop(0, 2)
-    def _(a):
-        edge_block(1, a, 1, self_part[0, a])
-
-    trade(3, msg.at[1, :, 1], in_y, up_y)
-    halos[0].wait_recv()
-    self_part[1] = mul(halo_x[...].reshape(128, 512), we[512:1024, :]).reshape(2, 64, 512)
-    @pl.loop(0, 2)
-    def _(b):
-        edge_block(0, 1, b, self_part[1, b])
-
-    trade(2, msg.at[0, 1], in_x, up_x)
+    for c in (1, 0):
+        halos[2 + c].wait_recv()
+        halos[c].wait_recv()
+        self_part[c] = mul(halo[c].reshape(128, 512), we[512:1024, :]).reshape(2, 64, 512)
+
+        @pl.loop(0, 2)
+        def _(d):
+            edge_block(d, 1 + d * (c - 1), c + d * (1 - c), self_part[c, d])
+
+        trade(6 + c, msg.at[1, c, 1], in_y.at[c], up_y)
+        trade(4 + c, msg.at[0, 1, c], in_x.at[c], up_x)
 
     for d in range(3):
         ef_t[:, 256 * d: 256 * d + 256] = ef[d].reshape(256, 512).T
-    hx_t[...] = halo_x[...].reshape(128, 512).T
-    hy_t[...] = halo_y[...].reshape(128, 512).T
+    hx_t[...] = jnp.concatenate([halo[0, 0], halo[1, 0]], axis=0).T
+    hy_t[...] = jnp.concatenate([halo[0, 1], halo[1, 1]], axis=0).T
     loads[4].wait()
     loads[5].wait()
 
-    halos[3].wait_recv()
-    halos[2].wait_recv()
-    for a, b in BLOCKS:
-        third = msg[2, a, b].astype(F32)
-        total = msg[0, a, b].astype(F32) + msg[1, a, b].astype(F32) + third
-        total = total - pltpu.roll(third, 1, 0)
-        total = total - (in_x[b] if a == 0 else msg[0, 0, b]).astype(F32)
-        total = total - (in_y[a] if b == 0 else msg[1, a, 0]).astype(F32)
-        summed[pl.ds(128 * a + 64 * b, 64), :] = total.astype(BF)
-    upper_part[...] = mul(summed[...], wn[...]).reshape(2, 2, 64, 512)
-    @pl.loop(0, 4)
-    def _(block):
-        a, b = block // 2, block % 2
-        value = upper_part[a, b]
-        s = sigmoid(value)
-        nn[a, b] = (nf[a, b].astype(F32) + value * s).astype(BF)
-        rows = pl.ds(pl.multiple_of(64 * block, 64), 64)
-        gu[rows, :] = (cot[a, b].astype(F32) * (s * (1.0 + value * (1.0 - s)))).astype(BF)
-
-    gs[...] = mul_nt(gu[...], wn[...]).astype(BF).reshape(2, 2, 64, 512)
-    trade(5, gs.at[:, 0], gs_y, down_y)
-    trade(4, gs.at[0], gs_x, down_x)
+    def node_blocks(blocks):
+        for a, b in blocks:
+            third = msg[2, a, b].astype(F32)
+            total = msg[0, a, b].astype(F32) + msg[1, a, b].astype(F32) + third
+            total = total - pltpu.roll(third, 1, 0)
+            total = total - (in_x[b] if a == 0 else msg[0, 0, b]).astype(F32)
+            total = total - (in_y[a] if b == 0 else msg[1, a, 0]).astype(F32)
+            summed[pl.ds(128 * a + 64 * b, 64), :] = total.astype(BF)
+
+    def node_update(low, high):
+        rows = pl.ds(64 * low, 64 * (high - low))
+        update[rows, :] = mul(summed[rows, :], wn[...])
+
+        @pl.loop(2 * low, 2 * high)
+        def _(half):
+            part = pl.ds(pl.multiple_of(32 * half, 32), 32)
+            value = update[part, :]
+            s = sigmoid(value)
+            nn[part, :] = (nf[part, :].astype(F32) + value * s).astype(BF)
+            gu[part, :] = (cot[part, :].astype(F32) * (s * (1.0 + value * (1.0 - s)))).astype(BF)
+
+        gs[rows, :] = mul_nt(gu[rows, :], wn[...]).astype(BF)
+
+    halos[7].wait_recv()
+    halos[5].wait_recv()
+    node_blocks(((0, 1), (1, 0), (1, 1)))
+    node_update(1, 4)
+    trade(11, gs.at[pl.ds(128, 64)], gs_y.at[1], down_y)
+    trade(9, gs.at[pl.ds(64, 64)], gs_x.at[1], down_x)
+    halos[6].wait_recv()
+    halos[4].wait_recv()
+    node_blocks(((0, 0),))
+    node_update(0, 1)
+    trade(10, gs.at[pl.ds(0, 64)], gs_y.at[0], down_y)
+    trade(8, gs.at[pl.ds(0, 64)], gs_x.at[0], down_x)
     store_nn = pltpu.make_async_copy(nn, nn_out, store_sem.at[0])
     store_nn.start()
 
@@ -325,26 +336,31 @@
     for c in range(2):
         node[c] = mul_tn(summed[...], gu[:, pl.ds(pl.multiple_of(mine + 128 * c, 128), 128)])
 
+    def gs_block(a, b):
+        return gs[pl.ds(128 * a + 64 * b, 64), :].astype(F32)
+
     def grad_block(d, a, b, above):
-        gp[d, a, b] = ((gs[a, b].astype(F32) - above) * pre[d, a, b]).astype(BF)
+        gp[d, a, b] = ((gs_block(a, b) - above) * pre[d, a, b]).astype(BF)
 
     for a, b in BLOCKS:
-        grad_block(2, a, b, pltpu.roll(gs[a, b].astype(F32), 63, 0))
+        grad_block(2, a, b, pltpu.roll(gs_block(a, b), 63, 0))
     for b in range(2):
-        grad_block(0, 0, b, gs[1, b].astype(F32))
+        grad_block(0, 0, b, gs_block(1, b))
     for a in range(2):
-        grad_block(1, a, 0, gs[a, 1].astype(F32))
+        grad_block(1, a, 0, gs_block(a, 1))
     swaps[0].wait_recv()
     for c in range(2):
         node[c] = node[c] + node_from[:, 128 * c: 128 * c + 128].astype(F32)
-    halos[5].wait_recv()
+    halos[11].wait_recv()
+    halos[10].wait_recv()
     for a in range(2):
         grad_block(1, a, 1, gs_y[a].astype(F32))
-    trade(7, gp.at[1, :, 1], gp_y, up_y)
-    halos[4].wait_recv()
+    trade(13, gp.at[1, :, 1], gp_y, up_y)
+    halos[9].wait_recv()
+    halos[8].wait_recv()
     for b in range(2):
         grad_block(0, 1, b, gs_x[b].astype(F32))
-    trade(6, gp.at[0, 1], gp_x, up_x)
+    trade(12, gp.at[0, 1], gp_x, up_x)
     for a, b in BLOCKS:
         rows = pl.ds(128 * a + 64 * b, 64)
         third = gp[2, a, b].astype(F32)
@@ -379,8 +395,8 @@
             edge[c, rows, :] = edge[c, rows, :] + edge_from[part, :, 128 * c: 128 * c + 128].astype(F32)
 
     def node_grads():
-        halos[6].wait_recv()
-        halos[7].wait_recv()
+        halos[12].wait_recv()
+        halos[13].wait_recv()
         for a, b in BLOCKS:
             total = pltpu.roll(gp[2, a, b].astype(F32), 1, 0)
             total = total + (gp[0, 0, b] if a else gp_x[b]).astype(F32)
@@ -391,7 +407,8 @@
         @pl.loop(0, 4)
         def _(block):
             a, b = block // 2, block % 2
-            ng[a, b] = (cot[a, b].astype(F32) + upper_part[a, b]).astype(BF)
+            part = pl.ds(pl.multiple_of(64 * block, 64), 64)
+            ng[part, :] = (cot[part, :].astype(F32) + upper_part[a, b]).astype(BF)
 
         pltpu.make_async_copy(ng, ng_out, store_sem.at[1]).start()
 
@@ -403,41 +420,49 @@
     pltpu.make_async_copy(ng, ng_out, store_sem.at[1]).wait()
 
 
+def settle_kernel(*refs):
+    copies = [pltpu.make_async_copy(refs[i], refs[4 + i], refs[8].at[i]) for i in range(4)]
+    for copy in copies:
+        copy.start()
+    for copy in copies:
+        copy.wait()
+
+
 def local(node_features, edge_features, open_faces, edge_weight, node_weight, cotangent):
     anywhere = pl.BlockSpec(memory_space=pltpu.HBM)
     vmem = pl.BlockSpec(memory_space=pltpu.VMEM)
-    nodes = (2, 2, 64, 512)
+    nodes, flat = (2, 2, 64, 512), (256, 512)
     plane = (2, 64, 512)
     new_nodes, node_grad, edge_part, node_part = pl.pallas_call(
         step_kernel,
         out_shape=(
-            jax.ShapeDtypeStruct(nodes, BF),
-            jax.ShapeDtypeStruct(nodes, BF),
+            jax.ShapeDtypeStruct(flat, BF),
+            jax.ShapeDtypeStruct(flat, BF),
             jax.ShapeDtypeStruct((12, 128), F32),
             jax.ShapeDtypeStruct((4, 128), F32),
         ),
         in_specs=[anywhere] * 6,
         out_specs=(anywhere, anywhere, vmem, vmem),
         scratch_shapes=[
-            pltpu.VMEM(nodes, BF),
+            pltpu.VMEM(flat, BF),
             pltpu.VMEM((3,) + nodes, BF),
             pltpu.VMEM((3, 2, 2, 64), jnp.int32),
             pltpu.VMEM((1536, 512), BF),
             pltpu.VMEM((512, 512), BF),
-            pltpu.VMEM(nodes, BF),
+            pltpu.VMEM(flat, BF),
             pltpu.VMEM((16, 64), F32),
             pltpu.VMEM((12, 64, 128), F32),
             pltpu.VMEM((3,) + nodes, F32),
             pltpu.VMEM(nodes, F32),
             pltpu.VMEM(nodes, F32),
-            pltpu.VMEM(plane, BF),
-            pltpu.VMEM(plane, BF),
+            pltpu.VMEM(nodes, BF),
+            pltpu.VMEM(flat, F32),
             pltpu.VMEM((3,) + nodes, BF),
             pltpu.VMEM(plane, BF),
             pltpu.VMEM(plane, BF),
             pltpu.VMEM((256, 512), BF),
             pltpu.VMEM((256, 512), BF),
-            pltpu.VMEM(nodes, BF),
+            pltpu.VMEM(flat, BF),
             pltpu.VMEM(plane, BF),
             pltpu.VMEM(plane, BF),
             pltpu.VMEM((3,) + nodes, BF),
@@ -449,12 +474,12 @@
             pltpu.VMEM((512, 128), BF),
             pltpu.VMEM((512, 128), BF),
             pltpu.VMEM((512, 768), BF),
-            pltpu.VMEM(nodes, BF),
-            pltpu.VMEM(nodes, BF),
+            pltpu.VMEM(flat, BF),
+            pltpu.VMEM(flat, BF),
             pltpu.SemaphoreType.DMA((6,)),
             pltpu.SemaphoreType.DMA((2,)),
-            pltpu.SemaphoreType.DMA((8,)),
-            pltpu.SemaphoreType.DMA((8,)),
+            pltpu.SemaphoreType.DMA((14,)),
+            pltpu.SemaphoreType.DMA((14,)),
             pltpu.VMEM((2, 1536, 128), F32),
             pltpu.VMEM((2, 512, 128), F32),
             pltpu.VMEM((3, 512, 256), BF),
@@ -466,8 +491,22 @@
         ] + scatter_scratch(),
         compiler_params=pltpu.CompilerParams(collective_id=0, has_side_effects=True, vmem_limit_bytes=64000000),
         name="mesh_step",
-    )(node_features, edge_features, open_faces, edge_weight, node_weight, cotangent)
-    return new_nodes, node_grad, edge_part.reshape(-1), node_part.reshape(-1)
+    )(node_features.reshape(flat), edge_features, open_faces, edge_weight, node_weight, cotangent.reshape(flat))
+    new_nodes, node_grad, edge_part, node_part = pl.pallas_call(
+        settle_kernel,
+        out_shape=(
+            jax.ShapeDtypeStruct(flat, BF),
+            jax.ShapeDtypeStruct(flat, BF),
+            jax.ShapeDtypeStruct((12, 128), F32),
+            jax.ShapeDtypeStruct((4, 128), F32),
+        ),
+        in_specs=[pl.BlockSpec(memory_space=pl.ANY)] * 4,
+        out_specs=(vmem,) * 4,
+        scratch_shapes=[pltpu.SemaphoreType.DMA((4,))],
+        compiler_params=pltpu.CompilerParams(vmem_limit_bytes=4 * 1024 * 1024),
+        name="settle",
+    )(new_nodes, node_grad, edge_part, node_part)
+    return new_nodes.reshape(nodes), node_grad.reshape(nodes), edge_part.reshape(-1), node_part.reshape(-1)
 
 
 def solution(mesh):

time: 64.9 us -> 61.2 us (0.943)
  local copies, waits for them, and re-layouts: 5.88 us -> 3.26 us
  Pallas kernels: 58.1 us -> 57.1 us
    unnamed x4 -> x8, local copies, waits for them, and re-layouts: 5.88 us -> 3.26 us
    pallas_call x1 -> x2, Pallas kernels: 58.1 us -> 57.1 us  [the longest x1 56.2 us: local(): pl.pallas_call(step_kernel, out_shape=(jax.ShapeDtypeStruct(flat, BF), ja...]
where the time goes in v3:
time: 61.2 us; the launch traced here: 61 us
  Pallas kernels  57.1 us (93%)
  local copies, waits for them, and re-layouts  3.26 us (5%)
  between operations  0.65 us (1%)
    pallas_call x1, Pallas kernels, local(): pl.pallas_call(step_kernel, out_shape=(jax.ShapeDtypeStruct(flat, BF), ja...  56.2 us
    unnamed x8, local copies, waits for them, and re-layouts  3.26 us

profile of v3, /device:TPU:1, one launch (start us, length us, event | category | flops | bytes accessed | tf_op | source)
XLA Modules:
  0.0 61.0 jit_solution(3463675288257840154)
XLA Ops:
  0.6 56.2 %mesh_step.1 = (bf16[256,512]{1,0:T(8,128)(2,1)}, bf16[256,512]{1,0:T(8,128)(2,1)}, f32[12,128]{1,0:T(8,128)}, f32[4,128]{1,0:T(4,128)}) custom-call(bf16[256,512]{1,0:T(8,128)(2,1)} %bitcast.6, bf16[3,2,2,64,512]{4,3,2,1,0:T(8,128)(2,1)} %ef_in.1, s32[3,2,2,64]{3,2,1,0:T(2,128)} %faces_in.1, bf16[1536,512]{1,0:T(8,128)(2,1)} %we_in.1, ...), custom_call_target="tpu_custom_call" | custom-call | tf_op jit(solution)/shard_map/mesh_step/pallas_call | solution.py:436
  56.8 0.0 copy-start
  56.8 0.9 %copy-done = bf16[256,512]{1,0:T(8,128)(2,1)S(1)} copy-done((bf16[256,512]{1,0:T(8,128)(2,1)S(1)}, bf16[256,512]{1,0:T(8,128)(2,1)}, u32[]{:S(2)}) %copy-start) | copy-done | bytes 262168
  57.8 0.0 copy-start.1
  57.8 0.9 %copy-done.1 = bf16[256,512]{1,0:T(8,128)(2,1)S(1)} copy-done((bf16[256,512]{1,0:T(8,128)(2,1)S(1)}, bf16[256,512]{1,0:T(8,128)(2,1)}, u32[]{:S(2)}) %copy-start.1) | copy-done | bytes 262168
  58.7 0.0 copy-start.2
  58.7 0.7 %copy-done.2 = f32[12,128]{1,0:T(8,128)S(1)} copy-done((f32[12,128]{1,0:T(8,128)S(1)}, f32[12,128]{1,0:T(8,128)}, u32[]{:S(2)}) %copy-start.2) | copy-done | bytes 6168
  59.4 0.0 copy-start.3
  59.4 0.7 %copy-done.3 = f32[4,128]{1,0:T(4,128)S(1)} copy-done((f32[4,128]{1,0:T(4,128)S(1)}, f32[4,128]{1,0:T(4,128)}, u32[]{:S(2)}) %copy-start.3) | copy-done | bytes 2072
  60.1 0.9 %settle.1 = (bf16[256,512]{1,0:T(8,128)(2,1)}, bf16[256,512]{1,0:T(8,128)(2,1)}, f32[12,128]{1,0:T(8,128)}, f32[4,128]{1,0:T(4,128)}) custom-call(bf16[256,512]{1,0:T(8,128)(2,1)S(1)} %copy-done, bf16[256,512]{1,0:T(8,128)(2,1)S(1)} %copy-done.1, f32[12,128]{1,0:T(8,128)S(1)} %copy-done.2, f32[4,128]{1,0:T(4,128)S(1)} %copy-done.3), custom_call_target="tpu_custom_call" | custom-call | tf_op jit(solution)/shard_map/settle/pallas_call | solution.py:495
Async XLA Ops:
  56.8 1.0 %copy-start = (bf16[256,512]{1,0:T(8,128)(2,1)S(1)}, bf16[256,512]{1,0:T(8,128)(2,1)}, u32[]{:S(2)}) copy-start(bf16[256,512]{1,0:T(8,128)(2,1)} %get-tuple-element.12.refs_0_) | copy-start | bytes 786436
  57.8 0.9 %copy-start.1 = (bf16[256,512]{1,0:T(8,128)(2,1)S(1)}, bf16[256,512]{1,0:T(8,128)(2,1)}, u32[]{:S(2)}) copy-start(bf16[256,512]{1,0:T(8,128)(2,1)} %get-tuple-element.13.refs_1_) | copy-start | bytes 786436
  58.7 0.7 %copy-start.2 = (f32[12,128]{1,0:T(8,128)S(1)}, f32[12,128]{1,0:T(8,128)}, u32[]{:S(2)}) copy-start(f32[12,128]{1,0:T(8,128)} %get-tuple-element.14.refs_2_) | copy-start | bytes 18436
  59.4 0.7 %copy-start.3 = (f32[4,128]{1,0:T(4,128)S(1)}, f32[4,128]{1,0:T(4,128)}, u32[]{:S(2)}) copy-start(f32[4,128]{1,0:T(4,128)} %get-tuple-element.15.refs_3_) | copy-start | bytes 6148

commit v4 on v3

--- a/solution.py
+++ b/solution.py
@@ -503,7 +503,7 @@
         in_specs=[pl.BlockSpec(memory_space=pl.ANY)] * 4,
         out_specs=(vmem,) * 4,
         scratch_shapes=[pltpu.SemaphoreType.DMA((4,))],
-        compiler_params=pltpu.CompilerParams(vmem_limit_bytes=4 * 1024 * 1024),
+        compiler_params=pltpu.CompilerParams(vmem_limit_bytes=64000000),
         name="settle",
     )(new_nodes, node_grad, edge_part, node_part)
     return new_nodes.reshape(nodes), node_grad.reshape(nodes), edge_part.reshape(-1), node_part.reshape(-1)

time: 61.2 us -> 58.8 us (0.961)
  local copies, waits for them, and re-layouts: 3.26 us -> 0 us
  Pallas kernels: 57.1 us -> 58 us
    unnamed x8 -> x0, local copies, waits for them, and re-layouts: 3.26 us -> none
    pallas_call x1, Pallas kernels: 0.87 us -> 1.86 us  [local(): pl.pallas_call(settle_kernel, out_shape=(jax.ShapeDtypeStruct(flat, BF),...]
where the time goes in v4:
time: 58.8 us; the launch traced here: 58.7 us
  Pallas kernels  58 us (99%)
  between operations  0.64 us (1%)
    pallas_call x1, Pallas kernels, local(): pl.pallas_call(step_kernel, out_shape=(jax.ShapeDtypeStruct(flat, BF), ja...  56.2 us
    pallas_call x1, Pallas kernels, local(): pl.pallas_call(settle_kernel, out_shape=(jax.ShapeDtypeStruct(flat, BF),...  1.86 us

profile of v4, /device:TPU:1, one launch (start us, length us, event | category | flops | bytes accessed | tf_op | source)
XLA Modules:
  0.0 58.7 jit_solution(15481782852068926830)
XLA Ops:
  0.6 56.2 %mesh_step.1 = (bf16[256,512]{1,0:T(8,128)(2,1)}, bf16[256,512]{1,0:T(8,128)(2,1)}, f32[12,128]{1,0:T(8,128)}, f32[4,128]{1,0:T(4,128)}) custom-call(bf16[256,512]{1,0:T(8,128)(2,1)} %bitcast.6, bf16[3,2,2,64,512]{4,3,2,1,0:T(8,128)(2,1)} %ef_in.1, s32[3,2,2,64]{3,2,1,0:T(2,128)} %faces_in.1, bf16[1536,512]{1,0:T(8,128)(2,1)} %we_in.1, ...), custom_call_target="tpu_custom_call" | custom-call | tf_op jit(solution)/shard_map/mesh_step/pallas_call | solution.py:436
  56.8 1.9 %settle.1 = (bf16[256,512]{1,0:T(8,128)(2,1)}, bf16[256,512]{1,0:T(8,128)(2,1)}, f32[12,128]{1,0:T(8,128)}, f32[4,128]{1,0:T(4,128)}) custom-call(bf16[256,512]{1,0:T(8,128)(2,1)} %get-tuple-element.12.refs_0_, bf16[256,512]{1,0:T(8,128)(2,1)} %get-tuple-element.13.refs_1_, f32[12,128]{1,0:T(8,128)} %get-tuple-element.14.refs_2_, ...), custom_call_target="tpu_custom_call" | custom-call | tf_op jit(solution)/shard_map/settle/pallas_call | solution.py:495
